TPU v7x, 256 devices: a whole 4x4x8 slice. The times are simulated.
256 devices in a mesh: blk: 32 (over x_lo, z, core), slab: 8 (over x_hi, y).
Axes of the slice: x: 4 (x_hi: 2, x_lo: 2; x = x_hi * 2 + x_lo), y: 4, z: 8, core: 2. Of those that a mesh axis runs over, the one named last changes fastest.
Arguments:
- tokens: bfloat16 [4194304, 128], P(('blk', 'slab')), may hold values from -6 to 6
- listed: int32 [16384, 3], P(('blk', 'slab')), may hold values from 0 to 1023, as said below
- centroids: bfloat16 [262144, 128], P('blk'), may hold values from -6 to 6
Outputs:
- refined: float32 [262144, 128], P(('blk', 'slab'))
- counts: float32 [262144], P(('blk', 'slab'))
Inputs may be any that keep to these rules, and one draw needn't show every extreme that they name: `listed`: in the rows of one device (64 token blocks), all ids of one owner group (id // 32) are equal, so a device names at most one block of each owner group. The three ids of a row are distinct.
All inputs are finite; a program needn't handle non-finite values.
Results may differ from a plain program's by a relative error of at most 0.00093.
Values may be sent and summed in bfloat16 or wider, within the bound.
No kernel may reach another device: no remote copies, remote signals or barrier semaphores. Data moves between devices by JAX's collectives and lax.ppermute only.
A program may use at most 128 MiB of HBM per device.

v0:
```python
import functools
import math

import jax
import jax.numpy as jnp
from jax import lax
from jax.experimental import pallas as pl
from jax.experimental.pallas import tpu as pltpu
from jax.sharding import Mesh
from jax.sharding import PartitionSpec as P

EMBED_WIDTH = 128
CENT_BLK = 256
TOK_BLK = 256
BPO = 32
MSG_ROWS = CENT_BLK + 8

SOFTMAX_TEMP = 0.1
PRIOR_WEIGHT = 4.0
EPSILON = 1e-06
EXP2_SCALE = math.log2(math.e) / (EMBED_WIDTH * SOFTMAX_TEMP)


def unit_rows(values):
    widened = values.astype(jnp.float32)
    return widened * lax.rsqrt(jnp.mean(widened * widened, axis=-1, keepdims=True) + EPSILON)


def split_counts(totals_a, totals_b):
    row = lax.broadcasted_iota(jnp.int32, (8, EMBED_WIDTH), 0)
    heads = jnp.where(row % 2 == 0, totals_a, totals_b)
    rounded = heads.astype(jnp.bfloat16).astype(jnp.float32)
    tails = heads - rounded
    tile = jnp.where(row < 2, rounded, jnp.where(row < 4, tails, 0.0))
    return tile.astype(jnp.bfloat16)


def prepare_kernel(tok_ref, unit_ref, turned_ref):
    tok = unit_rows(tok_ref[...]).astype(jnp.bfloat16)
    unit_ref[...] = tok
    for at in range(turned_ref.shape[0]):
        turned_ref[at] = tok[at * TOK_BLK:(at + 1) * TOK_BLK].T


def prepare(tokens, per_step=4):
    blocks = tokens.shape[0] // TOK_BLK
    per_step = math.gcd(per_step, blocks)
    rows = per_step * TOK_BLK
    return pl.pallas_call(
        prepare_kernel,
        grid=(blocks // per_step,),
        in_specs=[pl.BlockSpec((rows, EMBED_WIDTH), lambda i: (i, 0))],
        out_specs=(
            pl.BlockSpec((rows, EMBED_WIDTH), lambda i: (i, 0)),
            pl.BlockSpec((per_step, EMBED_WIDTH, TOK_BLK), lambda i: (i, 0, 0)),
        ),
        out_shape=(
            jax.ShapeDtypeStruct(tokens.shape, jnp.bfloat16),
            jax.ShapeDtypeStruct((blocks, EMBED_WIDTH, TOK_BLK), jnp.bfloat16),
        ),
        compiler_params=pltpu.CompilerParams(vmem_limit_bytes=56 << 20),
        cost_estimate=pl.CostEstimate(
            flops=tokens.size * 4, transcendentals=tokens.shape[0], bytes_accessed=tokens.size * 6
        ),
        name="prepare",
    )(tokens)


def attend_kernel(
    unroll, parts, slots, ids, unit_hbm, turned_hbm, recv_ref, out_ref,
    acc_ref, cnt_ref, exp_ref, inv_ref, cent_ref, unit_ref, turned_ref, unit_sems, turned_sems,
):
    blocks = turned_ref.shape[0]
    share = blocks // parts

    def unit_copy(part):
        rows = pl.ds(pl.multiple_of(part * share * TOK_BLK, TOK_BLK), share * TOK_BLK)
        return pltpu.make_async_copy(unit_hbm.at[rows], unit_ref.at[rows], unit_sems.at[part])

    def turned_copy(part):
        rows = pl.ds(part * share, share)
        return pltpu.make_async_copy(turned_hbm.at[rows], turned_ref.at[rows], turned_sems.at[part])

    for part in range(parts):
        unit_copy(part).start()
        turned_copy(part).start()
    acc_ref[...] = jnp.zeros_like(acc_ref)
    cnt_ref[...] = jnp.zeros_like(cnt_ref)
    exp_ref[1] = jnp.zeros(exp_ref.shape[1:], exp_ref.dtype)
    inv_ref[1] = jnp.zeros(inv_ref.shape[1:], inv_ref.dtype)
    quads, _, depth = recv_ref.shape[:3]
    cores = 2
    for quad in range(quads):
        def turn(at, carry):
            rows = recv_ref[quad, :, at].reshape(CENT_BLK, EMBED_WIDTH)
            cent_ref[((quad // cores) * depth + at) * cores + quad % cores] = rows.T
            return carry

        lax.fori_loop(0, depth, turn, 0, unroll=4)

    def spread(block, side):
        inverse = inv_ref[side]

        def piece(k):
            slot = slots[block * 3 + k]
            left = exp_ref[side, k, :, :128] * inverse
            right = exp_ref[side, k, :, 128:] * inverse
            weights = jnp.concatenate([left, right], axis=1)
            cnt_ref[slot] += jnp.sum(weights.reshape(TOK_BLK // 8, 8, CENT_BLK), axis=0)
            acc_ref[slot] += jnp.dot(
                turned_ref[block], weights.astype(jnp.bfloat16), preferred_element_type=jnp.float32
            )

        return piece

    def score(block, side):
        tok = unit_ref[pl.ds(pl.multiple_of(block * TOK_BLK, TOK_BLK), TOK_BLK), :]
        totals = []

        def piece(k):
            slot = slots[block * 3 + k]
            scores = jnp.dot(tok, cent_ref[slot], preferred_element_type=jnp.float32)
            grown = jnp.exp2(scores * EXP2_SCALE)
            exp_ref[side, k] = grown
            part = grown[:, :128] + grown[:, 128:]
            totals.append(part if not totals else totals.pop() + part)

        def close():
            total = jnp.sum(totals[0], axis=1, keepdims=True)
            inv_ref[side] = jnp.broadcast_to(1.0 / total, inv_ref.shape[1:])

        return piece, close

    def round_of(index, carry):
        @pl.when(index % (share // unroll) == 0)
        def _():
            unit_copy(index // (share // unroll)).wait()
            turned_copy(index // (share // unroll)).wait()

        for u in range(unroll):
            block = unroll * index + u
            piece_a, close = score(block, u % 2)
            piece_b = spread(jnp.maximum(block - 1, 0), (u + 1) % 2)
            for k in range(3):
                piece_a(k)
                piece_b(k)
            close()
        return carry

    lax.fori_loop(0, blocks // unroll, round_of, 0)
    piece = spread(blocks - 1, 1)
    for k in range(3):
        piece(k)
    finish(ids, out_ref, acc_ref, cnt_ref)


def finish(ids, out_ref, acc_ref, cnt_ref):
    row = lax.broadcasted_iota(jnp.int32, (8, EMBED_WIDTH), 0)

    def write(slot, carry):
        out_ref[slot, :128, :] = acc_ref[slot, :, :128].astype(jnp.bfloat16)
        out_ref[slot, 128:256, :] = acc_ref[slot, :, 128:].astype(jnp.bfloat16)
        counts = jnp.sum(cnt_ref[slot], axis=0, keepdims=True)
        tile = split_counts(counts[:, :128], counts[:, 128:])
        named = jnp.full(tile.shape, ids[slot].astype(jnp.float32))
        out_ref[slot, CENT_BLK:, :] = jnp.where(row == 4, named, tile.astype(jnp.float32)).astype(jnp.bfloat16)
        return carry

    lax.fori_loop(0, cnt_ref.shape[0], write, 0, unroll=4)


def attend(slots, ids, unit, turned, recv, unroll=4):
    owners = ids.shape[0]
    blocks = turned.shape[0]
    unroll = math.gcd(unroll, blocks)
    parts = math.gcd(4, blocks // unroll)
    pairs = blocks * 3 * TOK_BLK * CENT_BLK
    whole = lambda shape: pl.BlockSpec(
        shape, lambda i, s, n: (0,) * len(shape), pipeline_mode=pl.Buffered(1)
    )
    shape = (owners, MSG_ROWS, EMBED_WIDTH)
    return pl.pallas_call(
        functools.partial(attend_kernel, unroll, parts),
        grid_spec=pltpu.PrefetchScalarGridSpec(
            num_scalar_prefetch=2,
            grid=(1,),
            in_specs=[
                pl.BlockSpec(memory_space=pl.ANY),
                pl.BlockSpec(memory_space=pl.ANY),
                whole(recv.shape),
            ],
            out_specs=whole(shape),
            scratch_shapes=[
                pltpu.VMEM((owners, EMBED_WIDTH, CENT_BLK), jnp.float32),
                pltpu.VMEM((owners, 8, CENT_BLK), jnp.float32),
                pltpu.VMEM((2, 3, TOK_BLK, CENT_BLK), jnp.float32),
                pltpu.VMEM((2, TOK_BLK, 128), jnp.float32),
                pltpu.VMEM((owners, EMBED_WIDTH, CENT_BLK), jnp.bfloat16),
                pltpu.VMEM(unit.shape, jnp.bfloat16),
                pltpu.VMEM(turned.shape, jnp.bfloat16),
                pltpu.SemaphoreType.DMA((parts,)),
                pltpu.SemaphoreType.DMA((parts,)),
            ],
        ),
        out_shape=jax.ShapeDtypeStruct(shape, jnp.bfloat16),
        compiler_params=pltpu.CompilerParams(vmem_limit_bytes=48 << 20),
        cost_estimate=pl.CostEstimate(
            flops=pairs * EMBED_WIDTH * 4, transcendentals=pairs, bytes_accessed=unit.size * 6
        ),
        name="attend",
    )(slots, ids, unit, turned, recv)


def pick_kernel(asked, zpos, *refs):
    pieces, out_ref = refs[:-1], refs[-1]
    depth = out_ref.shape[1]
    half = pieces[0].shape[0]

    def fill(peer, carry):
        for at in range(depth):
            source = zpos[at]
            inner = jnp.maximum(asked[peer * depth + source], 0)
            low = jnp.where(inner < half, inner, inner - half)
            picked = jnp.where(inner < half, pieces[at][low], pieces[depth + at][low])
            out_ref[peer, source] = picked
        return carry

    lax.fori_loop(0, out_ref.shape[0], fill, 0, unroll=2)


def pick(asked, zpos, pieces, peers):
    depth = len(pieces) // 2
    rows = pieces[0].shape[1]
    shape = (peers, depth, rows, EMBED_WIDTH)
    return pl.pallas_call(
        pick_kernel,
        grid_spec=pltpu.PrefetchScalarGridSpec(
            num_scalar_prefetch=2,
            grid=(1,),
            in_specs=[
                pl.BlockSpec(p.shape, lambda i, s, n: (0, 0, 0), pipeline_mode=pl.Buffered(1))
                for p in pieces
            ],
            out_specs=pl.BlockSpec(shape, lambda i, s, n: (0, 0, 0, 0), pipeline_mode=pl.Buffered(1)),
        ),
        out_shape=jax.ShapeDtypeStruct(shape, jnp.bfloat16),
        compiler_params=pltpu.CompilerParams(vmem_limit_bytes=8 << 20),
        cost_estimate=pl.CostEstimate(flops=0, transcendentals=0, bytes_accessed=4 << 20),
        name="pick",
    )(asked, zpos, *pieces)


def gather_ring(low, high, axis):
    depth = lax.axis_size(axis)
    up = [(i, (i + 1) % depth) for i in range(depth)]
    down = [(i, (i - 1) % depth) for i in range(depth)]
    lows, highs = {0: low}, {0: high}
    rise, fall = depth // 2, (depth - 1) // 2
    for step in range(1, rise + 1):
        lows[step] = lax.ppermute(lows[step - 1], axis, up)
        highs[-step] = lax.ppermute(highs[1 - step], axis, down)
        if step <= fall:
            highs[step] = lax.ppermute(highs[step - 1], axis, up)
            lows[-step] = lax.ppermute(lows[1 - step], axis, down)
    lows = {away % depth: piece for away, piece in lows.items()}
    highs = {away % depth: piece for away, piece in highs.items()}
    return [lows[k] for k in range(depth)] + [highs[k] for k in range(depth)]


def collect_kernel(asked, back_ref, out_ref, acc_ref):
    acc_ref[...] = jnp.zeros_like(acc_ref)

    def add(source, carry):
        inner = asked[source]

        @pl.when(inner >= 0)
        def _():
            acc_ref[inner] += back_ref[source].astype(jnp.float32)

        return carry

    lax.fori_loop(0, back_ref.shape[0], add, 0)

    def write(inner, carry):
        out_ref[inner, :CENT_BLK, :] = acc_ref[inner, :CENT_BLK, :].astype(jnp.bfloat16)
        tile = acc_ref[inner, CENT_BLK:, :]
        totals = tile[0:2] + tile[2:4]
        out_ref[inner, CENT_BLK:, :] = split_counts(totals[0:1], totals[1:2])
        return carry

    lax.fori_loop(0, out_ref.shape[0], write, 0)


def collect(asked, back):
    shape = (BPO, MSG_ROWS, EMBED_WIDTH)
    return pl.pallas_call(
        collect_kernel,
        grid_spec=pltpu.PrefetchScalarGridSpec(
            num_scalar_prefetch=1,
            grid=(1,),
            in_specs=[pl.BlockSpec(back.shape, lambda i, s: (0, 0, 0), pipeline_mode=pl.Buffered(1))],
            out_specs=pl.BlockSpec(shape, lambda i, s: (0, 0, 0), pipeline_mode=pl.Buffered(1)),
            scratch_shapes=[pltpu.VMEM(shape, jnp.float32)],
        ),
        out_shape=jax.ShapeDtypeStruct(shape, jnp.bfloat16),
        compiler_params=pltpu.CompilerParams(vmem_limit_bytes=24 << 20),
        cost_estimate=pl.CostEstimate(
            flops=back.size, transcendentals=0, bytes_accessed=back.size * 4
        ),
        name="collect",
    )(asked, back)


OWNER = ("xlo", "z", "core")
PLANE = ("xlo", "core", "slab")


def shards(tokens, listed, centroids):
    slab_count = lax.axis_size("slab")
    slab_index = lax.axis_index("slab")
    depth = lax.axis_size("z")
    cores = lax.axis_size("core")
    quads = lax.axis_size("xlo") * cores
    owner_count = quads * depth
    peers = quads * slab_count
    share_blocks = BPO // slab_count
    share_rows = CENT_BLK // slab_count

    blocks = centroids.reshape(BPO, CENT_BLK, EMBED_WIDTH)
    piece = lax.dynamic_slice_in_dim(blocks, slab_index * share_rows, share_rows, 1)
    piece = unit_rows(piece).astype(jnp.bfloat16)
    pieces = gather_ring(piece[:BPO // 2], piece[BPO // 2:], "z")

    owner_ids = jnp.arange(owner_count, dtype=jnp.int32)
    group_of = listed // BPO
    inner_ids = listed % BPO
    matches = group_of[:, :, None] == owner_ids
    wanted = jnp.max(jnp.where(matches, inner_ids[:, :, None] + 1, 0), axis=(0, 1)) - 1
    by_quad = wanted.reshape(-1, depth, cores).transpose(0, 2, 1).reshape(quads, 1, depth)
    requests = jnp.broadcast_to(by_quad, (quads, slab_count, depth)).reshape(peers, 1, depth)
    asked = lax.all_to_all(requests, PLANE, split_axis=0, concat_axis=0, tiled=True)
    asked = asked.reshape(-1)

    zpos = (lax.axis_index("z") - jnp.arange(depth, dtype=jnp.int32)) % depth
    picked = pick(asked, zpos, pieces, peers)
    recv = lax.all_to_all(picked, PLANE, split_axis=0, concat_axis=0, tiled=True)
    recv = recv.reshape(quads, slab_count, depth, share_rows, EMBED_WIDTH)

    tokens, _ = lax.optimization_barrier((tokens, picked))
    unit, turned = prepare(tokens)
    partial = attend(group_of.reshape(-1), wanted, unit, turned, recv)
    back = lax.all_to_all(partial, OWNER, split_axis=0, concat_axis=0, tiled=True)
    own = collect(back[:, CENT_BLK + 4, 0].astype(jnp.int32), back)
    slabs = lax.all_to_all(own, "slab", split_axis=0, concat_axis=0, tiled=True)
    slabs = slabs.reshape(slab_count, share_blocks, MSG_ROWS, EMBED_WIDTH)

    totals = jnp.sum(slabs.astype(jnp.float32), axis=0)
    counts = (totals[:, CENT_BLK:CENT_BLK + 2] + totals[:, CENT_BLK + 2:CENT_BLK + 4]).reshape(-1)
    halves = totals[:, :CENT_BLK].reshape(share_blocks, 2, EMBED_WIDTH, CENT_BLK // 2)
    sums = halves.transpose(0, 1, 3, 2).reshape(-1, EMBED_WIDTH)
    rows = share_blocks * CENT_BLK
    mine = unit_rows(lax.dynamic_slice_in_dim(centroids, slab_index * rows, rows, 0))
    refined = (sums + PRIOR_WEIGHT * mine) / (counts[:, None] + PRIOR_WEIGHT)
    return refined, counts


def solution(mesh):
    owners, slabs = mesh.devices.shape
    split = Mesh(mesh.devices.reshape(2, owners // 4, 2, slabs), OWNER + ("slab",))
    every = OWNER + ("slab",)
    placed = (P(every, None), P(every, None), P(OWNER, None))
    return jax.shard_map(
        lambda *args: shards(*args),
        mesh=split,
        in_specs=placed,
        out_specs=(P(every, None), P(every)),
        check_vma=False,
    )
```

profile of v0, /device:TPU:1, one launch (start us, length us, event | category | flops | bytes accessed | tf_op | source)
XLA Modules:
  0.0 206.1 jit_solution(5321918559409665257)
XLA Ops:
  0.6 1.2 fusion
  1.8 1.2 fusion.1
  3.0 6.5 %collective-permute-start.10 = (bf16[16,32,128]{2,1,0:T(8,128)(2,1)S(1)}, bf16[16,32,128]{2,1,0:T(8,128)(2,1)S(1)}, u32[]{:S(2)}, u32[]{:S(2)}) collective-permute-start(bf16[16,32,128]{2,1,0:T(8,128)(2,1)S(1)} %get-tuple-element.8.refs_8_), channel_id=1, source_target_pairs={{0,112},{16,0},{32,16},{48,32},{64,48},{80,64},{96,80},{112,96},{1... | collective-permute-start | bytes 393224 | tf_op jit(solution)/shard_map/ppermute | solution.py:261
  9.5 0.0 collective-permute-start
  9.5 2.7 %collective-permute-start.4 = (bf16[16,32,128]{2,1,0:T(8,128)(2,1)S(1)}, bf16[16,32,128]{2,1,0:T(8,128)(2,1)S(1)}, u32[]{:S(2)}, u32[]{:S(2)}) collective-permute-start(bf16[16,32,128]{2,1,0:T(8,128)(2,1)S(1)} %get-tuple-element.9.refs_0_), channel_id=1, source_target_pairs={{0,112},{16,0},{32,16},{48,32},{64,48},{80,64},{96,80},{112,96},{1... | collective-permute-start | bytes 393224 | tf_op jit(solution)/shard_map/ppermute | solution.py:264
  12.2 0.0 collective-permute-start.7
  12.2 0.0 collective-permute-done.10.refs_15_
  12.2 2.9 %collective-permute-start.11 = (bf16[16,32,128]{2,1,0:T(8,128)(2,1)S(1)}, bf16[16,32,128]{2,1,0:T(8,128)(2,1)S(1)}, u32[]{:S(2)}, u32[]{:S(2)}) collective-permute-start(bf16[16,32,128]{2,1,0:T(8,128)(2,1)S(1)} %collective-permute-done.10.refs_15_), channel_id=1, source_target_pairs={{0,112},{16,0},{32,16},{48,32},{64,48},{80,64},{96,80},{112,96},{1... | collective-permute-start | bytes 393224 | tf_op jit(solution)/shard_map/ppermute | solution.py:261
  15.1 0.0 collective-permute-done.refs_1_
  15.1 0.0 collective-permute-start.1
  15.1 0.0 collective-permute-done.4.refs_7_
  15.1 2.7 %collective-permute-start.5 = (bf16[16,32,128]{2,1,0:T(8,128)(2,1)S(1)}, bf16[16,32,128]{2,1,0:T(8,128)(2,1)S(1)}, u32[]{:S(2)}, u32[]{:S(2)}) collective-permute-start(bf16[16,32,128]{2,1,0:T(8,128)(2,1)S(1)} %collective-permute-done.4.refs_7_), channel_id=1, source_target_pairs={{0,112},{16,0},{32,16},{48,32},{64,48},{80,64},{96,80},{112,96},{1... | collective-permute-start | bytes 393224 | tf_op jit(solution)/shard_map/ppermute | solution.py:264
  17.8 0.0 collective-permute-done.7.refs_9_
  17.8 0.0 collective-permute-start.8
  17.8 0.0 collective-permute-done.11.refs_14_
  17.8 2.7 %collective-permute-start.12 = (bf16[16,32,128]{2,1,0:T(8,128)(2,1)S(1)}, bf16[16,32,128]{2,1,0:T(8,128)(2,1)S(1)}, u32[]{:S(2)}, u32[]{:S(2)}) collective-permute-start(bf16[16,32,128]{2,1,0:T(8,128)(2,1)S(1)} %collective-permute-done.11.refs_14_), channel_id=1, source_target_pairs={{0,112},{16,0},{32,16},{48,32},{64,48},{80,64},{96,80},{112,96},{1... | collective-permute-start | bytes 393224 | tf_op jit(solution)/shard_map/ppermute | solution.py:261
  20.5 0.1 collective-permute-done.1.refs_2_
  20.6 0.0 collective-permute-start.2
  20.6 0.7 fusion.7
  21.3 0.1 select_reduce_fusion
  21.4 0.0 collective-permute-done.5.refs_6_
  21.4 2.7 %collective-permute-start.6 = (bf16[16,32,128]{2,1,0:T(8,128)(2,1)S(1)}, bf16[16,32,128]{2,1,0:T(8,128)(2,1)S(1)}, u32[]{:S(2)}, u32[]{:S(2)}) collective-permute-start(bf16[16,32,128]{2,1,0:T(8,128)(2,1)S(1)} %collective-permute-done.5.refs_6_), channel_id=1, source_target_pairs={{0,112},{16,0},{32,16},{48,32},{64,48},{80,64},{96,80},{112,96},{1... | collective-permute-start | bytes 393224 | tf_op jit(solution)/shard_map/ppermute | solution.py:264
  24.2 0.0 collective-permute-done.8.refs_10_
  24.2 0.0 collective-permute-start.9
  24.2 0.0 collective-permute-done.12.refs_13_
  24.2 3.0 %collective-permute-start.13 = (bf16[16,32,128]{2,1,0:T(8,128)(2,1)S(1)}, bf16[16,32,128]{2,1,0:T(8,128)(2,1)S(1)}, u32[]{:S(2)}, u32[]{:S(2)}) collective-permute-start(bf16[16,32,128]{2,1,0:T(8,128)(2,1)S(1)} %collective-permute-done.12.refs_13_), channel_id=1, source_target_pairs={{0,112},{16,0},{32,16},{48,32},{64,48},{80,64},{96,80},{112,96},{1... | collective-permute-start | bytes 393224 | tf_op jit(solution)/shard_map/ppermute | solution.py:261
  27.2 0.0 collective-permute-done.2.refs_3_
  27.2 0.0 collective-permute-start.3
  27.2 0.1 sub.20
  27.3 0.1 copy.23
  27.3 0.6 broadcast_in_dim.27
  28.0 11.6 %all-to-all-start = ((s32[32,1,8]{2,1,0:T(1,128)}), s32[32,1,8]{2,1,0:T(1,128)S(1)}, u32[]{:S(2)}, u32[]{:S(2)}) async-start(s32[32,1,8]{2,1,0:T(1,128)} %bitcast.2), calls=%async_computation | async-start | bytes 32768 | tf_op jit(solution)/shard_map/all_to_all | solution.py:341
  39.6 6.8 %all-to-all-done = s32[32,1,8]{2,1,0:T(1,128)S(1)} async-done(((s32[32,1,8]{2,1,0:T(1,128)}), s32[32,1,8]{2,1,0:T(1,128)S(1)}, u32[]{:S(2)}, u32[]{:S(2)}) %all-to-all-start) | async-done | bytes 1056 | tf_op jit(solution)/shard_map/all_to_all | solution.py:341
  46.4 0.5 broadcast.78
  47.0 0.7 reduce.5
  47.7 0.1 reshape.65.asked
  47.7 0.0 collective-permute-done.6.refs_5_
  47.7 0.0 collective-permute-done.9.refs_11_
  47.8 0.0 collective-permute-done.13.refs_12_
  47.8 0.0 collective-permute-done.3.refs_4_
  47.8 3.8 %pick.1 = bf16[32,8,32,128]{3,2,1,0:T(8,128)(2,1)} custom-call(s32[256]{0:T(256)S(1)} %reshape.65.asked, s32[8]{0:T(128)S(1)} %and_select_fusion.zpos, bf16[16,32,128]{2,1,0:T(8,128)(2,1)S(1)} %get-tuple-element.9.refs_0_, bf16[16,32,128]{2,1,0:T(8,128)(2,1)S(1)} %collective-permute-done.refs_1_, bf16[16,32,128]{2,1,0:T(8,128)(2,1)S(1)} %collective-permute-done.1.refs_2_, ...), custom_call_target="tpu_custom_call" | custom-call | bytes 4194304 | tf_op jit(solution)/shard_map/pick/pallas_call | solution.py:235
  51.6 4.6 %all-to-all-start.1 = ((bf16[32,8,32,128]{3,2,1,0:T(8,128)(2,1)}), bf16[32,8,32,128]{3,2,1,0:T(8,128)(2,1)S(1)}, u32[]{:S(2)}, u32[]{:S(2)}) async-start(bf16[32,8,32,128]{3,2,1,0:T(8,128)(2,1)} %pick.1), calls=%async_computation.1 | async-start | bytes 4194304 | tf_op jit(solution)/shard_map/all_to_all | solution.py:346
  56.2 0.1 copy.22
  56.3 0.1 reshape.63.slots
  56.4 12.3 %prepare.1 = (bf16[16384,128]{1,0:T(8,128)(2,1)}, bf16[64,128,256]{2,1,0:T(8,128)(2,1)}) custom-call(bf16[16384,128]{1,0:T(8,128)(2,1)} %tok_ref), custom_call_target="tpu_custom_call" | custom-call | flops 8388608 | bytes 12582912 | tf_op jit(solution)/shard_map/prepare/pallas_call | solution.py:49
  68.7 14.2 %all-to-all-done.1 = bf16[32,8,32,128]{3,2,1,0:T(8,128)(2,1)S(1)} async-done(((bf16[32,8,32,128]{3,2,1,0:T(8,128)(2,1)}), bf16[32,8,32,128]{3,2,1,0:T(8,128)(2,1)S(1)}, u32[]{:S(2)}, u32[]{:S(2)}) %all-to-all-start.1) | async-done | bytes 2097184 | tf_op jit(solution)/shard_map/all_to_all | solution.py:346
  82.9 25.6 %attend.1 = bf16[32,264,128]{2,1,0:T(8,128)(2,1)S(1)} custom-call(s32[192]{0:T(256)S(1)} %reshape.63.slots, s32[32]{0:T(128)S(1)} %broadcast_add_fusion.1.ids, bf16[16384,128]{1,0:T(8,128)(2,1)} %get-tuple-element.6.unit_hbm, bf16[64,128,256]{2,1,0:T(8,128)(2,1)} %get-tuple-element.7.turned_hbm, bf16[4,8,8,32,128]{4,3,2,1,0:T(8,128)(2,1)S(1)} %bitcast.13), custom_call_target="tpu_custom_call" | custom-call | flops 6442450944 | bytes 12582912 | tf_op jit(solution)/shard_map/attend/pallas_call | solution.py:182
  108.6 59.0 %all_to_all.20.back_ref = bf16[32,264,128]{2,1,0:T(8,128)(2,1)S(1)} all-to-all(bf16[32,264,128]{2,1,0:T(8,128)(2,1)S(1)} %attend.1), channel_id=1, replica_groups=mesh['xlo'=2,'z'=8,'core'=2,'slab'=8] {'xlo','z','core'}, dimensions={0} | all-to-all | bytes 4325376 | tf_op jit(solution)/shard_map/all_to_all | solution.py:352
  167.6 0.7 fusion.6.asked
  168.2 3.5 %collect.1 = bf16[32,264,128]{2,1,0:T(8,128)(2,1)} custom-call(s32[32]{0:T(128)S(1)} %fusion.6.asked, bf16[32,264,128]{2,1,0:T(8,128)(2,1)S(1)} %all_to_all.20.back_ref), custom_call_target="tpu_custom_call" | custom-call | flops 1081344 | bytes 4325376 | tf_op jit(solution)/shard_map/collect/pallas_call | solution.py:296
  171.7 4.8 %all-to-all-start.3 = ((bf16[32,264,128]{2,1,0:T(8,128)(2,1)}), bf16[32,264,128]{2,1,0:T(8,128)(2,1)S(1)}, u32[]{:S(2)}, u32[]{:S(2)}) async-start(bf16[32,264,128]{2,1,0:T(8,128)(2,1)} %collect.1), calls=%async_computation.3 | async-start | bytes 4325376 | tf_op jit(solution)/shard_map/all_to_all | solution.py:354
  176.5 1.2 fusion.2
  177.7 25.7 %all-to-all-done.3 = bf16[32,264,128]{2,1,0:T(8,128)(2,1)S(1)} async-done(((bf16[32,264,128]{2,1,0:T(8,128)(2,1)}), bf16[32,264,128]{2,1,0:T(8,128)(2,1)S(1)}, u32[]{:S(2)}, u32[]{:S(2)}) %all-to-all-start.3) | async-done | bytes 2162720 | tf_op jit(solution)/shard_map/all_to_all | solution.py:354
  203.4 0.3 convert_reduce_fusion
  203.8 0.0 copy-start
  203.8 0.2 copy.24
  204.0 2.1 %fusion.5 = f32[1024,128]{1,0:T(8,128)} fusion(f32[4,2,128,128]{3,2,1,0:T(8,128)S(1)} %copy.24, f32[1024]{0:T(1024)S(1)} %get-tuple-element.13, f32[1024]{0:T(1024)S(1)} %get-tuple-element.12, bf16[8192,128]{1,0:T(8,128)(2,1)} %param.5, s32[]{:T(128)S(6)} %select_n.33), kind=kLoop, calls=%fused_computation.10 | loop fusion | flops 655360 | bytes 1318916 | tf_op jit(solution)/shard_map/div | solution.py:363
  206.1 0.0 copy-done
  (7 shorter events, 0.1 us)
Async XLA Ops:
  3.0 9.2 %collective-permute-start.10 = (bf16[16,32,128]{2,1,0:T(8,128)(2,1)S(1)}, bf16[16,32,128]{2,1,0:T(8,128)(2,1)S(1)}, u32[]{:S(2)}, u32[]{:S(2)}) collective-permute-start(bf16[16,32,128]{2,1,0:T(8,128)(2,1)S(1)} %get-tuple-element.8.refs_8_), channel_id=1, source_target_pairs={{0,112},{16,0},{32,16},{48,32},{64,48},{80,64},{96,80},{112,96},{1... | collective-permute-start | bytes 393224 | tf_op jit(solution)/shard_map/ppermute | solution.py:261
  9.5 5.6 %collective-permute-start = (bf16[16,32,128]{2,1,0:T(8,128)(2,1)S(1)}, bf16[16,32,128]{2,1,0:T(8,128)(2,1)S(1)}, u32[]{:S(2)}, u32[]{:S(2)}) collective-permute-start(bf16[16,32,128]{2,1,0:T(8,128)(2,1)S(1)} %get-tuple-element.9.refs_0_), channel_id=1, source_target_pairs={{0,16},{16,32},{32,48},{48,64},{64,80},{80,96},{96,112},{112,0},{1... | collective-permute-start | bytes 393224 | tf_op jit(solution)/shard_map/ppermute | solution.py:260
  9.5 5.6 %collective-permute-start.4 = (bf16[16,32,128]{2,1,0:T(8,128)(2,1)S(1)}, bf16[16,32,128]{2,1,0:T(8,128)(2,1)S(1)}, u32[]{:S(2)}, u32[]{:S(2)}) collective-permute-start(bf16[16,32,128]{2,1,0:T(8,128)(2,1)S(1)} %get-tuple-element.9.refs_0_), channel_id=1, source_target_pairs={{0,112},{16,0},{32,16},{48,32},{64,48},{80,64},{96,80},{112,96},{1... | collective-permute-start | bytes 393224 | tf_op jit(solution)/shard_map/ppermute | solution.py:264
  12.2 5.6 %collective-permute-start.7 = (bf16[16,32,128]{2,1,0:T(8,128)(2,1)S(1)}, bf16[16,32,128]{2,1,0:T(8,128)(2,1)S(1)}, u32[]{:S(2)}, u32[]{:S(2)}) collective-permute-start(bf16[16,32,128]{2,1,0:T(8,128)(2,1)S(1)} %get-tuple-element.8.refs_8_), channel_id=1, source_target_pairs={{0,16},{16,32},{32,48},{48,64},{64,80},{80,96},{96,112},{112,0},{1... | collective-permute-start | bytes 393224 | tf_op jit(solution)/shard_map/ppermute | solution.py:263
  12.2 5.6 %collective-permute-start.11 = (bf16[16,32,128]{2,1,0:T(8,128)(2,1)S(1)}, bf16[16,32,128]{2,1,0:T(8,128)(2,1)S(1)}, u32[]{:S(2)}, u32[]{:S(2)}) collective-permute-start(bf16[16,32,128]{2,1,0:T(8,128)(2,1)S(1)} %collective-permute-done.10.refs_15_), channel_id=1, source_target_pairs={{0,112},{16,0},{32,16},{48,32},{64,48},{80,64},{96,80},{112,96},{1... | collective-permute-start | bytes 393224 | tf_op jit(solution)/shard_map/ppermute | solution.py:261
  15.1 5.5 %collective-permute-start.1 = (bf16[16,32,128]{2,1,0:T(8,128)(2,1)S(1)}, bf16[16,32,128]{2,1,0:T(8,128)(2,1)S(1)}, u32[]{:S(2)}, u32[]{:S(2)}) collective-permute-start(bf16[16,32,128]{2,1,0:T(8,128)(2,1)S(1)} %collective-permute-done.refs_1_), channel_id=1, source_target_pairs={{0,16},{16,32},{32,48},{48,64},{64,80},{80,96},{96,112},{112,0},{1... | collective-permute-start | bytes 393224 | tf_op jit(solution)/shard_map/ppermute | solution.py:260
  15.1 6.3 %collective-permute-start.5 = (bf16[16,32,128]{2,1,0:T(8,128)(2,1)S(1)}, bf16[16,32,128]{2,1,0:T(8,128)(2,1)S(1)}, u32[]{:S(2)}, u32[]{:S(2)}) collective-permute-start(bf16[16,32,128]{2,1,0:T(8,128)(2,1)S(1)} %collective-permute-done.4.refs_7_), channel_id=1, source_target_pairs={{0,112},{16,0},{32,16},{48,32},{64,48},{80,64},{96,80},{112,96},{1... | collective-permute-start | bytes 393224 | tf_op jit(solution)/shard_map/ppermute | solution.py:264
  17.8 6.4 %collective-permute-start.8 = (bf16[16,32,128]{2,1,0:T(8,128)(2,1)S(1)}, bf16[16,32,128]{2,1,0:T(8,128)(2,1)S(1)}, u32[]{:S(2)}, u32[]{:S(2)}) collective-permute-start(bf16[16,32,128]{2,1,0:T(8,128)(2,1)S(1)} %collective-permute-done.7.refs_9_), channel_id=1, source_target_pairs={{0,16},{16,32},{32,48},{48,64},{64,80},{80,96},{96,112},{112,0},{1... | collective-permute-start | bytes 393224 | tf_op jit(solution)/shard_map/ppermute | solution.py:263
  17.8 6.4 %collective-permute-start.12 = (bf16[16,32,128]{2,1,0:T(8,128)(2,1)S(1)}, bf16[16,32,128]{2,1,0:T(8,128)(2,1)S(1)}, u32[]{:S(2)}, u32[]{:S(2)}) collective-permute-start(bf16[16,32,128]{2,1,0:T(8,128)(2,1)S(1)} %collective-permute-done.11.refs_14_), channel_id=1, source_target_pairs={{0,112},{16,0},{32,16},{48,32},{64,48},{80,64},{96,80},{112,96},{1... | collective-permute-start | bytes 393224 | tf_op jit(solution)/shard_map/ppermute | solution.py:261
  20.6 6.6 %collective-permute-start.2 = (bf16[16,32,128]{2,1,0:T(8,128)(2,1)S(1)}, bf16[16,32,128]{2,1,0:T(8,128)(2,1)S(1)}, u32[]{:S(2)}, u32[]{:S(2)}) collective-permute-start(bf16[16,32,128]{2,1,0:T(8,128)(2,1)S(1)} %collective-permute-done.1.refs_2_), channel_id=1, source_target_pairs={{0,16},{16,32},{32,48},{48,64},{64,80},{80,96},{96,112},{112,0},{1... | collective-permute-start | bytes 393224 | tf_op jit(solution)/shard_map/ppermute | solution.py:260
  21.4 26.3 %collective-permute-start.6 = (bf16[16,32,128]{2,1,0:T(8,128)(2,1)S(1)}, bf16[16,32,128]{2,1,0:T(8,128)(2,1)S(1)}, u32[]{:S(2)}, u32[]{:S(2)}) collective-permute-start(bf16[16,32,128]{2,1,0:T(8,128)(2,1)S(1)} %collective-permute-done.5.refs_6_), channel_id=1, source_target_pairs={{0,112},{16,0},{32,16},{48,32},{64,48},{80,64},{96,80},{112,96},{1... | collective-permute-start | bytes 393224 | tf_op jit(solution)/shard_map/ppermute | solution.py:264
  24.2 23.6 %collective-permute-start.9 = (bf16[16,32,128]{2,1,0:T(8,128)(2,1)S(1)}, bf16[16,32,128]{2,1,0:T(8,128)(2,1)S(1)}, u32[]{:S(2)}, u32[]{:S(2)}) collective-permute-start(bf16[16,32,128]{2,1,0:T(8,128)(2,1)S(1)} %collective-permute-done.8.refs_10_), channel_id=1, source_target_pairs={{0,16},{16,32},{32,48},{48,64},{64,80},{80,96},{96,112},{112,0},{1... | collective-permute-start | bytes 393224 | tf_op jit(solution)/shard_map/ppermute | solution.py:263
  24.2 23.6 %collective-permute-start.13 = (bf16[16,32,128]{2,1,0:T(8,128)(2,1)S(1)}, bf16[16,32,128]{2,1,0:T(8,128)(2,1)S(1)}, u32[]{:S(2)}, u32[]{:S(2)}) collective-permute-start(bf16[16,32,128]{2,1,0:T(8,128)(2,1)S(1)} %collective-permute-done.12.refs_13_), channel_id=1, source_target_pairs={{0,112},{16,0},{32,16},{48,32},{64,48},{80,64},{96,80},{112,96},{1... | collective-permute-start | bytes 393224 | tf_op jit(solution)/shard_map/ppermute | solution.py:261
  27.2 20.6 %collective-permute-start.3 = (bf16[16,32,128]{2,1,0:T(8,128)(2,1)S(1)}, bf16[16,32,128]{2,1,0:T(8,128)(2,1)S(1)}, u32[]{:S(2)}, u32[]{:S(2)}) collective-permute-start(bf16[16,32,128]{2,1,0:T(8,128)(2,1)S(1)} %collective-permute-done.2.refs_3_), channel_id=1, source_target_pairs={{0,16},{16,32},{32,48},{48,64},{64,80},{80,96},{96,112},{112,0},{1... | collective-permute-start | bytes 393224 | tf_op jit(solution)/shard_map/ppermute | solution.py:260
  28.0 18.5 %all-to-all-start = ((s32[32,1,8]{2,1,0:T(1,128)}), s32[32,1,8]{2,1,0:T(1,128)S(1)}, u32[]{:S(2)}, u32[]{:S(2)}) async-start(s32[32,1,8]{2,1,0:T(1,128)} %bitcast.2), calls=%async_computation | async-start | bytes 32768 | tf_op jit(solution)/shard_map/all_to_all | solution.py:341
  51.6 31.4 %all-to-all-start.1 = ((bf16[32,8,32,128]{3,2,1,0:T(8,128)(2,1)}), bf16[32,8,32,128]{3,2,1,0:T(8,128)(2,1)S(1)}, u32[]{:S(2)}, u32[]{:S(2)}) async-start(bf16[32,8,32,128]{3,2,1,0:T(8,128)(2,1)} %pick.1), calls=%async_computation.1 | async-start | bytes 4194304 | tf_op jit(solution)/shard_map/all_to_all | solution.py:346
  171.7 31.7 %all-to-all-start.3 = ((bf16[32,264,128]{2,1,0:T(8,128)(2,1)}), bf16[32,264,128]{2,1,0:T(8,128)(2,1)S(1)}, u32[]{:S(2)}, u32[]{:S(2)}) async-start(bf16[32,264,128]{2,1,0:T(8,128)(2,1)} %collect.1), calls=%async_computation.3 | async-start | bytes 4325376 | tf_op jit(solution)/shard_map/all_to_all | solution.py:354
  203.8 2.4 %copy-start = (f32[4,2,128]{2,1,0:T(2,128)}, f32[4,2,128]{2,1,0:T(2,128)S(1)}, u32[]{:S(2)}) copy-start(f32[4,2,128]{2,1,0:T(2,128)S(1)} %slice_add_fusion) | copy-start | bytes 12292
where the time goes:
time: 207 us; the launch traced here: 206 us
  blocking collectives  59 us (29%)
  waiting for transfers between devices  46.9 us (23%)
  Pallas kernels  45.2 us (22%)
  starting transfers between devices  44.2 us (21%)
  other arithmetic  8.11 us (4%)
    all_to_all x1, blocking collectives, shards(): lax.all_to_all(partial, OWNER, split_axis=0, concat_axis=0, tiled=True)  59 us
    all_to_all x1, waiting for transfers between devices, shards(): slabs = lax.all_to_all(own, 'slab', split_axis=0, concat_axis=0, tiled=True)  25.7 us
    pallas_call x1, Pallas kernels, attend(): pl.pallas_call(functools.partial(attend_kernel, unroll, parts), grid_spec...  25.6 us
    ppermute x4, starting transfers between devices, gather_ring(): highs[-step] = lax.ppermute(highs[1 - step], axis, down)  15.1 us
    all_to_all x1, waiting for transfers between devices, shards(): lax.all_to_all(picked, PLANE, split_axis=0, concat_axis=0, tiled=True)  14.2 us
    pallas_call x1, Pallas kernels, prepare(): pl.pallas_call(prepare_kernel, grid=(blocks // per_step,), in_specs=[pl.B...  12.3 us
    all_to_all x1, starting transfers between devices, shards(): lax.all_to_all(requests, PLANE, split_axis=0, concat_axis=0, tiled=True)  11.6 us
    ppermute x3, starting transfers between devices, gather_ring(): lows[-step] = lax.ppermute(lows[1 - step], axis, down)  8.09 us
  transfers between devices with their start and end apart: 17, of which 4 were waited for; matrix products, arithmetic and copies ran while one was open for 2% of the time, Pallas kernels for 6%

commit v1 on v0

--- a/solution.py
+++ b/solution.py
@@ -42,7 +42,7 @@
         turned_ref[at] = tok[at * TOK_BLK:(at + 1) * TOK_BLK].T
 
 
-def prepare(tokens, per_step=4):
+def prepare(tokens, per_step=16):
     blocks = tokens.shape[0] // TOK_BLK
     per_step = math.gcd(per_step, blocks)
     rows = per_step * TOK_BLK
@@ -67,7 +67,7 @@
 
 
 def attend_kernel(
-    unroll, parts, slots, ids, unit_hbm, turned_hbm, recv_ref, out_ref,
+    unroll, parts, slots, ids, zpos, unit_hbm, turned_hbm, near_ref, far_ref, out_ref,
     acc_ref, cnt_ref, exp_ref, inv_ref, cent_ref, unit_ref, turned_ref, unit_sems, turned_sems,
 ):
     blocks = turned_ref.shape[0]
@@ -88,15 +88,17 @@
     cnt_ref[...] = jnp.zeros_like(cnt_ref)
     exp_ref[1] = jnp.zeros(exp_ref.shape[1:], exp_ref.dtype)
     inv_ref[1] = jnp.zeros(inv_ref.shape[1:], inv_ref.dtype)
-    quads, _, depth = recv_ref.shape[:3]
+    depth = near_ref.shape[2] + far_ref.shape[2]
     cores = 2
-    for quad in range(quads):
-        def turn(at, carry):
-            rows = recv_ref[quad, :, at].reshape(CENT_BLK, EMBED_WIDTH)
-            cent_ref[((quad // cores) * depth + at) * cores + quad % cores] = rows.T
+    for first, recv_ref in ((0, near_ref), (near_ref.shape[2], far_ref)):
+        def turn(quad, carry):
+            for at in range(recv_ref.shape[2]):
+                rows = recv_ref[quad, :, at].reshape(CENT_BLK, EMBED_WIDTH)
+                slot = ((quad // cores) * depth + zpos[first + at]) * cores + quad % cores
+                cent_ref[slot] = rows.T
             return carry
 
-        lax.fori_loop(0, depth, turn, 0, unroll=4)
+        lax.fori_loop(0, near_ref.shape[0], turn, 0)
 
     def spread(block, side):
         inverse = inv_ref[side]
@@ -169,25 +171,26 @@
     lax.fori_loop(0, cnt_ref.shape[0], write, 0, unroll=4)
 
 
-def attend(slots, ids, unit, turned, recv, unroll=4):
+def attend(slots, ids, zpos, unit, turned, near, far, unroll=4):
     owners = ids.shape[0]
     blocks = turned.shape[0]
     unroll = math.gcd(unroll, blocks)
     parts = math.gcd(4, blocks // unroll)
     pairs = blocks * 3 * TOK_BLK * CENT_BLK
     whole = lambda shape: pl.BlockSpec(
-        shape, lambda i, s, n: (0,) * len(shape), pipeline_mode=pl.Buffered(1)
+        shape, lambda i, s, n, z: (0,) * len(shape), pipeline_mode=pl.Buffered(1)
     )
     shape = (owners, MSG_ROWS, EMBED_WIDTH)
     return pl.pallas_call(
         functools.partial(attend_kernel, unroll, parts),
         grid_spec=pltpu.PrefetchScalarGridSpec(
-            num_scalar_prefetch=2,
+            num_scalar_prefetch=3,
             grid=(1,),
             in_specs=[
                 pl.BlockSpec(memory_space=pl.ANY),
                 pl.BlockSpec(memory_space=pl.ANY),
-                whole(recv.shape),
+                whole(near.shape),
+                whole(far.shape),
             ],
             out_specs=whole(shape),
             scratch_shapes=[
@@ -208,63 +211,57 @@
             flops=pairs * EMBED_WIDTH * 4, transcendentals=pairs, bytes_accessed=unit.size * 6
         ),
         name="attend",
-    )(slots, ids, unit, turned, recv)
-
-
-def pick_kernel(asked, zpos, *refs):
+    )(slots, ids, zpos, unit, turned, near, far)
+
+
+def pick_kernel(asked, zpos, depth, *refs):
     pieces, out_ref = refs[:-1], refs[-1]
-    depth = out_ref.shape[1]
-    half = pieces[0].shape[0]
 
     def fill(peer, carry):
-        for at in range(depth):
-            source = zpos[at]
-            inner = jnp.maximum(asked[peer * depth + source], 0)
-            low = jnp.where(inner < half, inner, inner - half)
-            picked = jnp.where(inner < half, pieces[at][low], pieces[depth + at][low])
-            out_ref[peer, source] = picked
-        return carry
-
-    lax.fori_loop(0, out_ref.shape[0], fill, 0, unroll=2)
+        for at in range(len(pieces)):
+            inner = asked[peer * depth[0] + zpos[at]]
+            out_ref[peer, at] = pieces[at][jnp.maximum(inner, 0)]
+        return carry
+
+    lax.fori_loop(0, out_ref.shape[0], fill, 0, unroll=4)
 
 
 def pick(asked, zpos, pieces, peers):
-    depth = len(pieces) // 2
     rows = pieces[0].shape[1]
-    shape = (peers, depth, rows, EMBED_WIDTH)
+    shape = (peers, len(pieces), rows, EMBED_WIDTH)
+    depth = jnp.full((1,), asked.shape[0] // peers, jnp.int32)
     return pl.pallas_call(
         pick_kernel,
         grid_spec=pltpu.PrefetchScalarGridSpec(
-            num_scalar_prefetch=2,
+            num_scalar_prefetch=3,
             grid=(1,),
             in_specs=[
-                pl.BlockSpec(p.shape, lambda i, s, n: (0, 0, 0), pipeline_mode=pl.Buffered(1))
+                pl.BlockSpec(p.shape, lambda i, s, n, d: (0, 0, 0), pipeline_mode=pl.Buffered(1))
                 for p in pieces
             ],
-            out_specs=pl.BlockSpec(shape, lambda i, s, n: (0, 0, 0, 0), pipeline_mode=pl.Buffered(1)),
+            out_specs=pl.BlockSpec(
+                shape, lambda i, s, n, d: (0, 0, 0, 0), pipeline_mode=pl.Buffered(1)
+            ),
         ),
         out_shape=jax.ShapeDtypeStruct(shape, jnp.bfloat16),
         compiler_params=pltpu.CompilerParams(vmem_limit_bytes=8 << 20),
         cost_estimate=pl.CostEstimate(flops=0, transcendentals=0, bytes_accessed=4 << 20),
         name="pick",
-    )(asked, zpos, *pieces)
-
-
-def gather_ring(low, high, axis):
+    )(asked, zpos, depth, *pieces)
+
+
+def gather_ring(piece, axis):
     depth = lax.axis_size(axis)
     up = [(i, (i + 1) % depth) for i in range(depth)]
     down = [(i, (i - 1) % depth) for i in range(depth)]
-    lows, highs = {0: low}, {0: high}
+    pieces = {0: piece}
     rise, fall = depth // 2, (depth - 1) // 2
     for step in range(1, rise + 1):
-        lows[step] = lax.ppermute(lows[step - 1], axis, up)
-        highs[-step] = lax.ppermute(highs[1 - step], axis, down)
+        pieces[step] = lax.ppermute(pieces[step - 1], axis, up)
         if step <= fall:
-            highs[step] = lax.ppermute(highs[step - 1], axis, up)
-            lows[-step] = lax.ppermute(lows[1 - step], axis, down)
-    lows = {away % depth: piece for away, piece in lows.items()}
-    highs = {away % depth: piece for away, piece in highs.items()}
-    return [lows[k] for k in range(depth)] + [highs[k] for k in range(depth)]
+            pieces[-step] = lax.ppermute(pieces[1 - step], axis, down)
+    pieces = {away % depth: piece for away, piece in pieces.items()}
+    return [pieces[k] for k in range(depth)]
 
 
 def collect_kernel(asked, back_ref, out_ref, acc_ref):
@@ -329,7 +326,7 @@
     blocks = centroids.reshape(BPO, CENT_BLK, EMBED_WIDTH)
     piece = lax.dynamic_slice_in_dim(blocks, slab_index * share_rows, share_rows, 1)
     piece = unit_rows(piece).astype(jnp.bfloat16)
-    pieces = gather_ring(piece[:BPO // 2], piece[BPO // 2:], "z")
+    pieces = gather_ring(piece, "z")
 
     owner_ids = jnp.arange(owner_count, dtype=jnp.int32)
     group_of = listed // BPO
@@ -341,14 +338,19 @@
     asked = lax.all_to_all(requests, PLANE, split_axis=0, concat_axis=0, tiled=True)
     asked = asked.reshape(-1)
 
-    zpos = (lax.axis_index("z") - jnp.arange(depth, dtype=jnp.int32)) % depth
-    picked = pick(asked, zpos, pieces, peers)
-    recv = lax.all_to_all(picked, PLANE, split_axis=0, concat_axis=0, tiled=True)
-    recv = recv.reshape(quads, slab_count, depth, share_rows, EMBED_WIDTH)
+    reach = depth // 4
+    order = sorted(range(depth), key=lambda away: (min(away, depth - away), away))
+    zpos = (lax.axis_index("z") - jnp.array(order, jnp.int32)) % depth
+    split = 2 * reach + 1
+    received = []
+    for part in (slice(0, split), slice(split, depth)):
+        picked = pick(asked, zpos[part], [pieces[away] for away in order[part]], peers)
+        recv = lax.all_to_all(picked, PLANE, split_axis=0, concat_axis=0, tiled=True)
+        received.append(recv.reshape(quads, slab_count, -1, share_rows, EMBED_WIDTH))
 
     tokens, _ = lax.optimization_barrier((tokens, picked))
     unit, turned = prepare(tokens)
-    partial = attend(group_of.reshape(-1), wanted, unit, turned, recv)
+    partial = attend(group_of.reshape(-1), wanted, zpos, unit, turned, *received)
     back = lax.all_to_all(partial, OWNER, split_axis=0, concat_axis=0, tiled=True)
     own = collect(back[:, CENT_BLK + 4, 0].astype(jnp.int32), back)
     slabs = lax.all_to_all(own, "slab", split_axis=0, concat_axis=0, tiled=True)

time: 207 us -> 207 us (level)
  waiting for transfers between devices: 46.9 us -> 57.1 us
  starting transfers between devices: 44.2 us -> 37.9 us
  Pallas kernels: 45.2 us -> 39.7 us
    ppermute x14 -> x7, waiting for transfers between devices: 0.16 us -> 19.1 us  [the longest x4 19 us: gather_ring(): pieces[step] = lax.ppermute(pieces[step - 1], axis, up)]
    ppermute x14 -> x7, starting transfers between devices: 23.2 us -> 12 us  [the longest x3 9.37 us: gather_ring(): pieces[-step] = lax.ppermute(pieces[1 - step], axis, down)]
    all_to_all x1 -> x2, starting transfers between devices: 4.61 us -> 13.1 us  [shards(): lax.all_to_all(picked, PLANE, split_axis=0, concat_axis=0, tiled=True)]
    all_to_all x1 -> x2, waiting for transfers between devices: 14.2 us -> 6.1 us  [shards(): lax.all_to_all(picked, PLANE, split_axis=0, concat_axis=0, tiled=True)]
    pallas_call x1, Pallas kernels: 12.3 us -> 6.99 us  [prepare(): pl.pallas_call(prepare_kernel, grid=(blocks // per_step,), in_specs=[pl.B...]
    all_to_all x1, starting transfers between devices: 11.6 us -> 8.9 us  [shards(): lax.all_to_all(requests, PLANE, split_axis=0, concat_axis=0, tiled=True)]
  transfers between devices with their start and end apart: 17 -> 11, of which waited for: 4 -> 7; matrix products, arithmetic and copies ran while one was open for 2% -> 2% of each run, Pallas kernels for 6% -> 4%
where the time goes in v1:
time: 207 us
  blocking collectives  60.4 us (29%)
  waiting for transfers between devices  57.1 us (28%)
  Pallas kernels  39.7 us (19%)
  starting transfers between devices  37.9 us (18%)
  other arithmetic  8.77 us (4%)
    all_to_all x1, blocking collectives, shards(): lax.all_to_all(partial, OWNER, split_axis=0, concat_axis=0, tiled=True)  60.4 us
    all_to_all x1, waiting for transfers between devices, shards(): slabs = lax.all_to_all(own, 'slab', split_axis=0, concat_axis=0, tiled=True)  25.7 us
    pallas_call x1, Pallas kernels, attend(): pl.pallas_call(functools.partial(attend_kernel, unroll, parts), grid_spec...  25.6 us
    ppermute x4, waiting for transfers between devices, gather_ring(): pieces[step] = lax.ppermute(pieces[step - 1], axis, up)  19 us
    all_to_all x2, starting transfers between devices, shards(): lax.all_to_all(picked, PLANE, split_axis=0, concat_axis=0, tiled=True)  13.1 us
    ppermute x3, starting transfers between devices, gather_ring(): pieces[-step] = lax.ppermute(pieces[1 - step], axis, down)  9.37 us
    all_to_all x1, starting transfers between devices, shards(): lax.all_to_all(requests, PLANE, split_axis=0, concat_axis=0, tiled=True)  8.9 us
    pallas_call x1, Pallas kernels, prepare(): pl.pallas_call(prepare_kernel, grid=(blocks // per_step,), in_specs=[pl.B...  6.99 us
  transfers between devices with their start and end apart: 11, of which 7 were waited for; matrix products, arithmetic and copies ran while one was open for 2% of the time, Pallas kernels for 4%

profile of v1, /device:TPU:1, one launch (start us, length us, event | category | flops | bytes accessed | tf_op | source)
XLA Modules:
  0.0 206.6 jit_solution(17694732761740775483)
XLA Ops:
  0.6 1.2 fusion
  1.8 1.2 fusion.1.refs_0_
  3.0 2.5 %collective-permute-start = (bf16[32,32,128]{2,1,0:T(8,128)(2,1)S(1)}, bf16[32,32,128]{2,1,0:T(8,128)(2,1)S(1)}, u32[]{:S(2)}, u32[]{:S(2)}) collective-permute-start(bf16[32,32,128]{2,1,0:T(8,128)(2,1)S(1)} %fusion.1.refs_0_), channel_id=1, source_target_pairs={{0,16},{16,32},{32,48},{48,64},{64,80},{80,96},{96,112},{112,0},{1... | collective-permute-start | bytes 786440 | tf_op jit(solution)/shard_map/ppermute | solution.py:260
  5.5 4.0 %collective-permute-start.3 = (bf16[32,32,128]{2,1,0:T(8,128)(2,1)S(1)}, bf16[32,32,128]{2,1,0:T(8,128)(2,1)S(1)}, u32[]{:S(2)}, u32[]{:S(2)}) collective-permute-start(bf16[32,32,128]{2,1,0:T(8,128)(2,1)S(1)} %fusion.1.refs_0_), channel_id=1, source_target_pairs={{0,112},{16,0},{32,16},{48,32},{64,48},{80,64},{96,80},{112,96},{1... | collective-permute-start | bytes 786440 | tf_op jit(solution)/shard_map/ppermute | solution.py:262
  9.6 0.7 fusion.7
  10.2 0.1 select_reduce_fusion
  10.4 5.1 %collective-permute-done.refs_1_ = bf16[32,32,128]{2,1,0:T(8,128)(2,1)S(1)} collective-permute-done((bf16[32,32,128]{2,1,0:T(8,128)(2,1)S(1)}, bf16[32,32,128]{2,1,0:T(8,128)(2,1)S(1)}, u32[]{:S(2)}, u32[]{:S(2)}) %collective-permute-start) | collective-permute-done | bytes 262176 | tf_op jit(solution)/shard_map/ppermute | solution.py:260
  15.5 0.0 collective-permute-start.1
  15.5 0.0 collective-permute-done.3.refs_2_
  15.5 2.7 %collective-permute-start.4 = (bf16[32,32,128]{2,1,0:T(8,128)(2,1)S(1)}, bf16[32,32,128]{2,1,0:T(8,128)(2,1)S(1)}, u32[]{:S(2)}, u32[]{:S(2)}) collective-permute-start(bf16[32,32,128]{2,1,0:T(8,128)(2,1)S(1)} %collective-permute-done.3.refs_2_), channel_id=1, source_target_pairs={{0,112},{16,0},{32,16},{48,32},{64,48},{80,64},{96,80},{112,96},{1... | collective-permute-start | bytes 786440 | tf_op jit(solution)/shard_map/ppermute | solution.py:262
  18.2 0.1 sub.22
  18.2 0.1 copy.24
  18.3 0.6 broadcast_in_dim.27
  19.0 8.9 %all-to-all-start = ((s32[32,1,8]{2,1,0:T(1,128)}), s32[32,1,8]{2,1,0:T(1,128)S(1)}, u32[]{:S(2)}, u32[]{:S(2)}) async-start(s32[32,1,8]{2,1,0:T(1,128)} %bitcast.2), calls=%async_computation | async-start | bytes 32768 | tf_op jit(solution)/shard_map/all_to_all | solution.py:338
  27.9 0.7 and_select_fusion.zpos
  28.5 6.2 %all-to-all-done = s32[32,1,8]{2,1,0:T(1,128)S(1)} async-done(((s32[32,1,8]{2,1,0:T(1,128)}), s32[32,1,8]{2,1,0:T(1,128)S(1)}, u32[]{:S(2)}, u32[]{:S(2)}) %all-to-all-start) | async-done | bytes 1056 | tf_op jit(solution)/shard_map/all_to_all | solution.py:338
  34.7 0.5 broadcast.78
  35.2 0.7 reduce.5
  35.9 0.1 reshape.68.asked
  36.0 0.0 collective-permute-done.1.refs_3_
  36.0 0.0 collective-permute-done.4.refs_4_
  36.0 2.0 pick.3
  38.0 4.4 %all-to-all-start.1 = ((bf16[32,5,32,128]{3,2,1,0:T(8,128)(2,1)}), bf16[32,5,32,128]{3,2,1,0:T(8,128)(2,1)S(1)}, u32[]{:S(2)}, u32[]{:S(2)}) async-start(bf16[32,5,32,128]{3,2,1,0:T(8,128)(2,1)} %pick.3), calls=%async_computation.1 | async-start | bytes 2621440 | tf_op jit(solution)/shard_map/all_to_all | solution.py:348
  42.4 0.1 collective-permute-start.2
  42.5 2.7 %collective-permute-start.5 = (bf16[32,32,128]{2,1,0:T(8,128)(2,1)S(1)}, bf16[32,32,128]{2,1,0:T(8,128)(2,1)S(1)}, u32[]{:S(2)}, u32[]{:S(2)}) collective-permute-start(bf16[32,32,128]{2,1,0:T(8,128)(2,1)S(1)} %collective-permute-done.4.refs_4_), channel_id=1, source_target_pairs={{0,112},{16,0},{32,16},{48,32},{64,48},{80,64},{96,80},{112,96},{1... | collective-permute-start | bytes 786440 | tf_op jit(solution)/shard_map/ppermute | solution.py:262
  45.1 6.1 %collective-permute-done.2.refs_0_ = bf16[32,32,128]{2,1,0:T(8,128)(2,1)S(1)} collective-permute-done((bf16[32,32,128]{2,1,0:T(8,128)(2,1)S(1)}, bf16[32,32,128]{2,1,0:T(8,128)(2,1)S(1)}, u32[]{:S(2)}, u32[]{:S(2)}) %collective-permute-start.2) | collective-permute-done | bytes 262176 | tf_op jit(solution)/shard_map/ppermute | solution.py:260
  51.2 0.0 collective-permute-start.6
  51.2 0.1 slice.18.zpos
  51.3 0.0 collective-permute-done.5.refs_1_
  51.3 7.8 %collective-permute-done.6.refs_2_ = bf16[32,32,128]{2,1,0:T(8,128)(2,1)S(1)} collective-permute-done((bf16[32,32,128]{2,1,0:T(8,128)(2,1)S(1)}, bf16[32,32,128]{2,1,0:T(8,128)(2,1)S(1)}, u32[]{:S(2)}, u32[]{:S(2)}) %collective-permute-start.6) | collective-permute-done | bytes 262176 | tf_op jit(solution)/shard_map/ppermute | solution.py:260
  59.2 1.7 pick.2
  60.9 0.3 all-to-all-done.1
  61.2 8.7 %all-to-all-start.2 = ((bf16[32,3,32,128]{3,2,1,0:T(8,128)(2,1)}), bf16[32,3,32,128]{3,2,1,0:T(8,128)(2,1)S(1)}, u32[]{:S(2)}, u32[]{:S(2)}) async-start(bf16[32,3,32,128]{3,2,1,0:T(8,128)(2,1)} %pick.2), calls=%async_computation.2 | async-start | bytes 1572864 | tf_op jit(solution)/shard_map/all_to_all | solution.py:348
  69.9 0.1 copy.23
  70.0 0.1 reshape.66.slots
  70.1 7.0 %prepare.1 = (bf16[16384,128]{1,0:T(8,128)(2,1)}, bf16[64,128,256]{2,1,0:T(8,128)(2,1)}) custom-call(bf16[16384,128]{1,0:T(8,128)(2,1)} %tok_ref), custom_call_target="tpu_custom_call" | custom-call | flops 8388608 | bytes 12582912 | tf_op jit(solution)/shard_map/prepare/pallas_call | solution.py:49
  77.1 5.8 %all-to-all-done.2 = bf16[32,3,32,128]{3,2,1,0:T(8,128)(2,1)S(1)} async-done(((bf16[32,3,32,128]{3,2,1,0:T(8,128)(2,1)}), bf16[32,3,32,128]{3,2,1,0:T(8,128)(2,1)S(1)}, u32[]{:S(2)}, u32[]{:S(2)}) %all-to-all-start.2) | async-done | bytes 786464 | tf_op jit(solution)/shard_map/all_to_all | solution.py:348
  82.9 25.6 %attend.1 = bf16[32,264,128]{2,1,0:T(8,128)(2,1)S(1)} custom-call(s32[192]{0:T(256)S(1)} %reshape.66.slots, s32[32]{0:T(128)S(1)} %broadcast_add_fusion.1.ids, s32[8]{0:T(128)S(1)} %and_select_fusion.zpos, bf16[16384,128]{1,0:T(8,128)(2,1)} %get-tuple-element.6.unit_hbm, bf16[64,128,256]{2,1,0:T(8,128)(2,1)} %get-tuple-element.7.turned_hbm, ...), custom_call_target="tpu_custom_call" | custom-call | flops 6442450944 | bytes 12582912 | tf_op jit(solution)/shard_map/attend/pallas_call | solution.py:184
  108.5 60.4 %all_to_all.25.back_ref = bf16[32,264,128]{2,1,0:T(8,128)(2,1)S(1)} all-to-all(bf16[32,264,128]{2,1,0:T(8,128)(2,1)S(1)} %attend.1), channel_id=1, replica_groups=mesh['xlo'=2,'z'=8,'core'=2,'slab'=8] {'xlo','z','core'}, dimensions={0} | all-to-all | bytes 4325376 | tf_op jit(solution)/shard_map/all_to_all | solution.py:354
  168.9 0.7 fusion.6.asked
  169.6 3.5 %collect.1 = bf16[32,264,128]{2,1,0:T(8,128)(2,1)} custom-call(s32[32]{0:T(128)S(1)} %fusion.6.asked, bf16[32,264,128]{2,1,0:T(8,128)(2,1)S(1)} %all_to_all.25.back_ref), custom_call_target="tpu_custom_call" | custom-call | flops 1081344 | bytes 4325376 | tf_op jit(solution)/shard_map/collect/pallas_call | solution.py:293
  173.1 3.9 %all-to-all-start.4 = ((bf16[32,264,128]{2,1,0:T(8,128)(2,1)}), bf16[32,264,128]{2,1,0:T(8,128)(2,1)S(1)}, u32[]{:S(2)}, u32[]{:S(2)}) async-start(bf16[32,264,128]{2,1,0:T(8,128)(2,1)} %collect.1), calls=%async_computation.4 | async-start | bytes 4325376 | tf_op jit(solution)/shard_map/all_to_all | solution.py:356
  177.0 1.2 fusion.2
  178.1 25.7 %all-to-all-done.4 = bf16[32,264,128]{2,1,0:T(8,128)(2,1)S(1)} async-done(((bf16[32,264,128]{2,1,0:T(8,128)(2,1)}), bf16[32,264,128]{2,1,0:T(8,128)(2,1)S(1)}, u32[]{:S(2)}, u32[]{:S(2)}) %all-to-all-start.4) | async-done | bytes 2162720 | tf_op jit(solution)/shard_map/all_to_all | solution.py:356
  203.9 0.3 convert_reduce_fusion
  204.2 0.0 copy-start
  204.2 0.2 copy.25
  204.4 2.1 %fusion.5 = f32[1024,128]{1,0:T(8,128)} fusion(f32[4,2,128,128]{3,2,1,0:T(8,128)S(1)} %copy.25, f32[1024]{0:T(1024)S(1)} %broadcast_add_fusion, f32[1024]{0:T(1024)S(1)} %add_rsqrt_fusion.1, bf16[8192,128]{1,0:T(8,128)(2,1)} %param.6, s32[]{:T(128)S(6)} %select_n.33), kind=kLoop, calls=%fused_computation.10 | loop fusion | flops 655360 | bytes 1318916 | tf_op jit(solution)/shard_map/div | solution.py:365
  206.6 0.0 copy-done
  (6 shorter events, 0.1 us)
Async XLA Ops:
  3.0 12.5 %collective-permute-start = (bf16[32,32,128]{2,1,0:T(8,128)(2,1)S(1)}, bf16[32,32,128]{2,1,0:T(8,128)(2,1)S(1)}, u32[]{:S(2)}, u32[]{:S(2)}) collective-permute-start(bf16[32,32,128]{2,1,0:T(8,128)(2,1)S(1)} %fusion.1.refs_0_), channel_id=1, source_target_pairs={{0,16},{16,32},{32,48},{48,64},{64,80},{80,96},{96,112},{112,0},{1... | collective-permute-start | bytes 786440 | tf_op jit(solution)/shard_map/ppermute | solution.py:260
  5.5 10.0 %collective-permute-start.3 = (bf16[32,32,128]{2,1,0:T(8,128)(2,1)S(1)}, bf16[32,32,128]{2,1,0:T(8,128)(2,1)S(1)}, u32[]{:S(2)}, u32[]{:S(2)}) collective-permute-start(bf16[32,32,128]{2,1,0:T(8,128)(2,1)S(1)} %fusion.1.refs_0_), channel_id=1, source_target_pairs={{0,112},{16,0},{32,16},{48,32},{64,48},{80,64},{96,80},{112,96},{1... | collective-permute-start | bytes 786440 | tf_op jit(solution)/shard_map/ppermute | solution.py:262
  15.5 20.5 %collective-permute-start.1 = (bf16[32,32,128]{2,1,0:T(8,128)(2,1)S(1)}, bf16[32,32,128]{2,1,0:T(8,128)(2,1)S(1)}, u32[]{:S(2)}, u32[]{:S(2)}) collective-permute-start(bf16[32,32,128]{2,1,0:T(8,128)(2,1)S(1)} %collective-permute-done.refs_1_), channel_id=1, source_target_pairs={{0,16},{16,32},{32,48},{48,64},{64,80},{80,96},{96,112},{112,0},{1... | collective-permute-start | bytes 786440 | tf_op jit(solution)/shard_map/ppermute | solution.py:260
  15.5 20.5 %collective-permute-start.4 = (bf16[32,32,128]{2,1,0:T(8,128)(2,1)S(1)}, bf16[32,32,128]{2,1,0:T(8,128)(2,1)S(1)}, u32[]{:S(2)}, u32[]{:S(2)}) collective-permute-start(bf16[32,32,128]{2,1,0:T(8,128)(2,1)S(1)} %collective-permute-done.3.refs_2_), channel_id=1, source_target_pairs={{0,112},{16,0},{32,16},{48,32},{64,48},{80,64},{96,80},{112,96},{1... | collective-permute-start | bytes 786440 | tf_op jit(solution)/shard_map/ppermute | solution.py:262
  19.0 15.8 %all-to-all-start = ((s32[32,1,8]{2,1,0:T(1,128)}), s32[32,1,8]{2,1,0:T(1,128)S(1)}, u32[]{:S(2)}, u32[]{:S(2)}) async-start(s32[32,1,8]{2,1,0:T(1,128)} %bitcast.2), calls=%async_computation | async-start | bytes 32768 | tf_op jit(solution)/shard_map/all_to_all | solution.py:338
  38.0 23.2 %all-to-all-start.1 = ((bf16[32,5,32,128]{3,2,1,0:T(8,128)(2,1)}), bf16[32,5,32,128]{3,2,1,0:T(8,128)(2,1)S(1)}, u32[]{:S(2)}, u32[]{:S(2)}) async-start(bf16[32,5,32,128]{3,2,1,0:T(8,128)(2,1)} %pick.3), calls=%async_computation.1 | async-start | bytes 2621440 | tf_op jit(solution)/shard_map/all_to_all | solution.py:348
  42.4 8.9 %collective-permute-start.2 = (bf16[32,32,128]{2,1,0:T(8,128)(2,1)S(1)}, bf16[32,32,128]{2,1,0:T(8,128)(2,1)S(1)}, u32[]{:S(2)}, u32[]{:S(2)}) collective-permute-start(bf16[32,32,128]{2,1,0:T(8,128)(2,1)S(1)} %collective-permute-done.1.refs_3_), channel_id=1, source_target_pairs={{0,16},{16,32},{32,48},{48,64},{64,80},{80,96},{96,112},{112,0},{1... | collective-permute-start | bytes 786440 | tf_op jit(solution)/shard_map/ppermute | solution.py:260
  42.5 8.8 %collective-permute-start.5 = (bf16[32,32,128]{2,1,0:T(8,128)(2,1)S(1)}, bf16[32,32,128]{2,1,0:T(8,128)(2,1)S(1)}, u32[]{:S(2)}, u32[]{:S(2)}) collective-permute-start(bf16[32,32,128]{2,1,0:T(8,128)(2,1)S(1)} %collective-permute-done.4.refs_4_), channel_id=1, source_target_pairs={{0,112},{16,0},{32,16},{48,32},{64,48},{80,64},{96,80},{112,96},{1... | collective-permute-start | bytes 786440 | tf_op jit(solution)/shard_map/ppermute | solution.py:262
  51.2 7.9 %collective-permute-start.6 = (bf16[32,32,128]{2,1,0:T(8,128)(2,1)S(1)}, bf16[32,32,128]{2,1,0:T(8,128)(2,1)S(1)}, u32[]{:S(2)}, u32[]{:S(2)}) collective-permute-start(bf16[32,32,128]{2,1,0:T(8,128)(2,1)S(1)} %collective-permute-done.2.refs_0_), channel_id=1, source_target_pairs={{0,16},{16,32},{32,48},{48,64},{64,80},{80,96},{96,112},{112,0},{1... | collective-permute-start | bytes 786440 | tf_op jit(solution)/shard_map/ppermute | solution.py:260
  61.2 21.7 %all-to-all-start.2 = ((bf16[32,3,32,128]{3,2,1,0:T(8,128)(2,1)}), bf16[32,3,32,128]{3,2,1,0:T(8,128)(2,1)S(1)}, u32[]{:S(2)}, u32[]{:S(2)}) async-start(bf16[32,3,32,128]{3,2,1,0:T(8,128)(2,1)} %pick.2), calls=%async_computation.2 | async-start | bytes 1572864 | tf_op jit(solution)/shard_map/all_to_all | solution.py:348
  173.1 30.8 %all-to-all-start.4 = ((bf16[32,264,128]{2,1,0:T(8,128)(2,1)}), bf16[32,264,128]{2,1,0:T(8,128)(2,1)S(1)}, u32[]{:S(2)}, u32[]{:S(2)}) async-start(bf16[32,264,128]{2,1,0:T(8,128)(2,1)} %collect.1), calls=%async_computation.4 | async-start | bytes 4325376 | tf_op jit(solution)/shard_map/all_to_all | solution.py:356
  204.2 2.4 %copy-start = (f32[4,2,128]{2,1,0:T(2,128)}, f32[4,2,128]{2,1,0:T(2,128)S(1)}, u32[]{:S(2)}) copy-start(f32[4,2,128]{2,1,0:T(2,128)S(1)} %slice_add_fusion) | copy-start | bytes 12292

commit v2 on v1

--- a/solution.py
+++ b/solution.py
@@ -171,7 +171,7 @@
     lax.fori_loop(0, cnt_ref.shape[0], write, 0, unroll=4)
 
 
-def attend(slots, ids, zpos, unit, turned, near, far, unroll=4):
+def attend(slots, ids, zpos, unit, turned, near, far, unroll=8):
     owners = ids.shape[0]
     blocks = turned.shape[0]
     unroll = math.gcd(unroll, blocks)
@@ -269,14 +269,11 @@
 
     def add(source, carry):
         inner = asked[source]
-
-        @pl.when(inner >= 0)
-        def _():
-            acc_ref[inner] += back_ref[source].astype(jnp.float32)
-
-        return carry
-
-    lax.fori_loop(0, back_ref.shape[0], add, 0)
+        sent = back_ref[source].astype(jnp.float32)
+        acc_ref[jnp.maximum(inner, 0)] += jnp.where(inner >= 0, sent, 0.0)
+        return carry
+
+    lax.fori_loop(0, back_ref.shape[0], add, 0, unroll=4)
 
     def write(inner, carry):
         out_ref[inner, :CENT_BLK, :] = acc_ref[inner, :CENT_BLK, :].astype(jnp.bfloat16)
@@ -285,7 +282,7 @@
         out_ref[inner, CENT_BLK:, :] = split_counts(totals[0:1], totals[1:2])
         return carry
 
-    lax.fori_loop(0, out_ref.shape[0], write, 0)
+    lax.fori_loop(0, out_ref.shape[0], write, 0, unroll=4)
 
 
 def collect(asked, back):
@@ -338,6 +335,8 @@
     asked = lax.all_to_all(requests, PLANE, split_axis=0, concat_axis=0, tiled=True)
     asked = asked.reshape(-1)
 
+    tokens, _ = lax.optimization_barrier((tokens, asked))
+    unit, turned = prepare(tokens)
     reach = depth // 4
     order = sorted(range(depth), key=lambda away: (min(away, depth - away), away))
     zpos = (lax.axis_index("z") - jnp.array(order, jnp.int32)) % depth
@@ -348,8 +347,6 @@
         recv = lax.all_to_all(picked, PLANE, split_axis=0, concat_axis=0, tiled=True)
         received.append(recv.reshape(quads, slab_count, -1, share_rows, EMBED_WIDTH))
 
-    tokens, _ = lax.optimization_barrier((tokens, picked))
-    unit, turned = prepare(tokens)
     partial = attend(group_of.reshape(-1), wanted, zpos, unit, turned, *received)
     back = lax.all_to_all(partial, OWNER, split_axis=0, concat_axis=0, tiled=True)
     own = collect(back[:, CENT_BLK + 4, 0].astype(jnp.int32), back)

time: 207 us -> 206 us (level)
  no operation moved by 1% of the time
where the time goes in v2:
time: 206 us
  blocking collectives  60.4 us (29%)
  waiting for transfers between devices  57.1 us (28%)
  Pallas kernels  38.7 us (19%)
  starting transfers between devices  37.9 us (18%)
  other arithmetic  8.77 us (4%)
    all_to_all x1, blocking collectives, shards(): lax.all_to_all(partial, OWNER, split_axis=0, concat_axis=0, tiled=True)  60.4 us
    all_to_all x1, waiting for transfers between devices, shards(): slabs = lax.all_to_all(own, 'slab', split_axis=0, concat_axis=0, tiled=True)  25.7 us
    pallas_call x1, Pallas kernels, attend(): pl.pallas_call(functools.partial(attend_kernel, unroll, parts), grid_spec...  25 us
    ppermute x4, waiting for transfers between devices, gather_ring(): pieces[step] = lax.ppermute(pieces[step - 1], axis, up)  19 us
    all_to_all x2, starting transfers between devices, shards(): lax.all_to_all(picked, PLANE, split_axis=0, concat_axis=0, tiled=True)  13.1 us
    ppermute x3, starting transfers between devices, gather_ring(): pieces[-step] = lax.ppermute(pieces[1 - step], axis, down)  9.37 us
    all_to_all x1, starting transfers between devices, shards(): lax.all_to_all(requests, PLANE, split_axis=0, concat_axis=0, tiled=True)  8.9 us
    pallas_call x1, Pallas kernels, prepare(): pl.pallas_call(prepare_kernel, grid=(blocks // per_step,), in_specs=[pl.B...  6.99 us
  transfers between devices with their start and end apart: 11, of which 7 were waited for; matrix products, arithmetic and copies ran while one was open for 2% of the time, Pallas kernels for 4%

profile of v2, /device:TPU:1, one launch (start us, length us, event | category | flops | bytes accessed | tf_op | source)
XLA Modules:
  0.0 205.6 jit_solution(5160054341396144916)
XLA Ops:
  0.6 1.2 fusion
  1.8 1.2 fusion.1.refs_0_
  3.0 2.5 %collective-permute-start = (bf16[32,32,128]{2,1,0:T(8,128)(2,1)S(1)}, bf16[32,32,128]{2,1,0:T(8,128)(2,1)S(1)}, u32[]{:S(2)}, u32[]{:S(2)}) collective-permute-start(bf16[32,32,128]{2,1,0:T(8,128)(2,1)S(1)} %fusion.1.refs_0_), channel_id=1, source_target_pairs={{0,16},{16,32},{32,48},{48,64},{64,80},{80,96},{96,112},{112,0},{1... | collective-permute-start | bytes 786440 | tf_op jit(solution)/shard_map/ppermute | solution.py:260
  5.5 4.0 %collective-permute-start.1 = (bf16[32,32,128]{2,1,0:T(8,128)(2,1)S(1)}, bf16[32,32,128]{2,1,0:T(8,128)(2,1)S(1)}, u32[]{:S(2)}, u32[]{:S(2)}) collective-permute-start(bf16[32,32,128]{2,1,0:T(8,128)(2,1)S(1)} %fusion.1.refs_0_), channel_id=1, source_target_pairs={{0,112},{16,0},{32,16},{48,32},{64,48},{80,64},{96,80},{112,96},{1... | collective-permute-start | bytes 786440 | tf_op jit(solution)/shard_map/ppermute | solution.py:262
  9.6 0.7 fusion.7
  10.2 0.1 select_reduce_fusion
  10.4 5.1 %collective-permute-done.refs_1_ = bf16[32,32,128]{2,1,0:T(8,128)(2,1)S(1)} collective-permute-done((bf16[32,32,128]{2,1,0:T(8,128)(2,1)S(1)}, bf16[32,32,128]{2,1,0:T(8,128)(2,1)S(1)}, u32[]{:S(2)}, u32[]{:S(2)}) %collective-permute-start) | collective-permute-done | bytes 262176 | tf_op jit(solution)/shard_map/ppermute | solution.py:260
  15.5 0.0 collective-permute-start.2
  15.5 0.0 collective-permute-done.1.refs_2_
  15.5 2.7 %collective-permute-start.3 = (bf16[32,32,128]{2,1,0:T(8,128)(2,1)S(1)}, bf16[32,32,128]{2,1,0:T(8,128)(2,1)S(1)}, u32[]{:S(2)}, u32[]{:S(2)}) collective-permute-start(bf16[32,32,128]{2,1,0:T(8,128)(2,1)S(1)} %collective-permute-done.1.refs_2_), channel_id=1, source_target_pairs={{0,112},{16,0},{32,16},{48,32},{64,48},{80,64},{96,80},{112,96},{1... | collective-permute-start | bytes 786440 | tf_op jit(solution)/shard_map/ppermute | solution.py:262
  18.2 0.1 sub.22
  18.2 0.1 copy.24
  18.3 0.6 broadcast_in_dim.27
  19.0 8.9 %all-to-all-start = ((s32[32,1,8]{2,1,0:T(1,128)}), s32[32,1,8]{2,1,0:T(1,128)S(1)}, u32[]{:S(2)}, u32[]{:S(2)}) async-start(s32[32,1,8]{2,1,0:T(1,128)} %bitcast.2), calls=%async_computation | async-start | bytes 32768 | tf_op jit(solution)/shard_map/all_to_all | solution.py:335
  27.9 0.7 and_select_fusion.zpos
  28.5 6.2 %all-to-all-done = s32[32,1,8]{2,1,0:T(1,128)S(1)} async-done(((s32[32,1,8]{2,1,0:T(1,128)}), s32[32,1,8]{2,1,0:T(1,128)S(1)}, u32[]{:S(2)}, u32[]{:S(2)}) %all-to-all-start) | async-done | bytes 1056 | tf_op jit(solution)/shard_map/all_to_all | solution.py:335
  34.7 0.5 broadcast.78
  35.2 0.7 reduce.5
  35.9 0.1 reshape.68.asked
  36.0 0.0 collective-permute-done.2.refs_3_
  36.0 0.0 collective-permute-done.3.refs_4_
  36.0 2.0 pick.2
  38.0 4.4 %all-to-all-start.1 = ((bf16[32,5,32,128]{3,2,1,0:T(8,128)(2,1)}), bf16[32,5,32,128]{3,2,1,0:T(8,128)(2,1)S(1)}, u32[]{:S(2)}, u32[]{:S(2)}) async-start(bf16[32,5,32,128]{3,2,1,0:T(8,128)(2,1)} %pick.2), calls=%async_computation.1 | async-start | bytes 2621440 | tf_op jit(solution)/shard_map/all_to_all | solution.py:347
  42.4 0.1 collective-permute-start.4
  42.5 2.7 %collective-permute-start.5 = (bf16[32,32,128]{2,1,0:T(8,128)(2,1)S(1)}, bf16[32,32,128]{2,1,0:T(8,128)(2,1)S(1)}, u32[]{:S(2)}, u32[]{:S(2)}) collective-permute-start(bf16[32,32,128]{2,1,0:T(8,128)(2,1)S(1)} %collective-permute-done.3.refs_4_), channel_id=1, source_target_pairs={{0,112},{16,0},{32,16},{48,32},{64,48},{80,64},{96,80},{112,96},{1... | collective-permute-start | bytes 786440 | tf_op jit(solution)/shard_map/ppermute | solution.py:262
  45.1 6.1 %collective-permute-done.4.refs_0_ = bf16[32,32,128]{2,1,0:T(8,128)(2,1)S(1)} collective-permute-done((bf16[32,32,128]{2,1,0:T(8,128)(2,1)S(1)}, bf16[32,32,128]{2,1,0:T(8,128)(2,1)S(1)}, u32[]{:S(2)}, u32[]{:S(2)}) %collective-permute-start.4) | collective-permute-done | bytes 262176 | tf_op jit(solution)/shard_map/ppermute | solution.py:260
  51.2 0.0 collective-permute-start.6
  51.2 0.1 slice.19.zpos
  51.3 0.0 collective-permute-done.5.refs_1_
  51.3 7.8 %collective-permute-done.6.refs_2_ = bf16[32,32,128]{2,1,0:T(8,128)(2,1)S(1)} collective-permute-done((bf16[32,32,128]{2,1,0:T(8,128)(2,1)S(1)}, bf16[32,32,128]{2,1,0:T(8,128)(2,1)S(1)}, u32[]{:S(2)}, u32[]{:S(2)}) %collective-permute-start.6) | collective-permute-done | bytes 262176 | tf_op jit(solution)/shard_map/ppermute | solution.py:260
  59.2 1.7 pick.3
  60.9 0.3 all-to-all-done.1
  61.2 8.7 %all-to-all-start.2 = ((bf16[32,3,32,128]{3,2,1,0:T(8,128)(2,1)}), bf16[32,3,32,128]{3,2,1,0:T(8,128)(2,1)S(1)}, u32[]{:S(2)}, u32[]{:S(2)}) async-start(bf16[32,3,32,128]{3,2,1,0:T(8,128)(2,1)} %pick.3), calls=%async_computation.2 | async-start | bytes 1572864 | tf_op jit(solution)/shard_map/all_to_all | solution.py:347
  69.9 0.1 copy.23
  70.0 0.1 reshape.66.slots
  70.1 7.0 %prepare.1 = (bf16[16384,128]{1,0:T(8,128)(2,1)}, bf16[64,128,256]{2,1,0:T(8,128)(2,1)}) custom-call(bf16[16384,128]{1,0:T(8,128)(2,1)} %tok_ref), custom_call_target="tpu_custom_call" | custom-call | flops 8388608 | bytes 12582912 | tf_op jit(solution)/shard_map/prepare/pallas_call | solution.py:49
  77.1 5.8 %all-to-all-done.2 = bf16[32,3,32,128]{3,2,1,0:T(8,128)(2,1)S(1)} async-done(((bf16[32,3,32,128]{3,2,1,0:T(8,128)(2,1)}), bf16[32,3,32,128]{3,2,1,0:T(8,128)(2,1)S(1)}, u32[]{:S(2)}, u32[]{:S(2)}) %all-to-all-start.2) | async-done | bytes 786464 | tf_op jit(solution)/shard_map/all_to_all | solution.py:347
  82.9 25.0 %attend.1 = bf16[32,264,128]{2,1,0:T(8,128)(2,1)S(1)} custom-call(s32[192]{0:T(256)S(1)} %reshape.66.slots, s32[32]{0:T(128)S(1)} %broadcast_add_fusion.1.ids, s32[8]{0:T(128)S(1)} %and_select_fusion.zpos, bf16[16384,128]{1,0:T(8,128)(2,1)} %get-tuple-element.6.unit_hbm, bf16[64,128,256]{2,1,0:T(8,128)(2,1)} %get-tuple-element.7.turned_hbm, ...), custom_call_target="tpu_custom_call" | custom-call | flops 6442450944 | bytes 12582912 | tf_op jit(solution)/shard_map/attend/pallas_call | solution.py:184
  107.9 60.4 %all_to_all.25.back_ref = bf16[32,264,128]{2,1,0:T(8,128)(2,1)S(1)} all-to-all(bf16[32,264,128]{2,1,0:T(8,128)(2,1)S(1)} %attend.1), channel_id=1, replica_groups=mesh['xlo'=2,'z'=8,'core'=2,'slab'=8] {'xlo','z','core'}, dimensions={0} | all-to-all | bytes 4325376 | tf_op jit(solution)/shard_map/all_to_all | solution.py:351
  168.4 0.7 fusion.6.asked
  169.0 3.0 %collect.1 = bf16[32,264,128]{2,1,0:T(8,128)(2,1)} custom-call(s32[32]{0:T(128)S(1)} %fusion.6.asked, bf16[32,264,128]{2,1,0:T(8,128)(2,1)S(1)} %all_to_all.25.back_ref), custom_call_target="tpu_custom_call" | custom-call | flops 1081344 | bytes 4325376 | tf_op jit(solution)/shard_map/collect/pallas_call | solution.py:290
  172.0 3.9 %all-to-all-start.4 = ((bf16[32,264,128]{2,1,0:T(8,128)(2,1)}), bf16[32,264,128]{2,1,0:T(8,128)(2,1)S(1)}, u32[]{:S(2)}, u32[]{:S(2)}) async-start(bf16[32,264,128]{2,1,0:T(8,128)(2,1)} %collect.1), calls=%async_computation.4 | async-start | bytes 4325376 | tf_op jit(solution)/shard_map/all_to_all | solution.py:353
  176.0 1.2 fusion.2
  177.1 25.7 %all-to-all-done.4 = bf16[32,264,128]{2,1,0:T(8,128)(2,1)S(1)} async-done(((bf16[32,264,128]{2,1,0:T(8,128)(2,1)}), bf16[32,264,128]{2,1,0:T(8,128)(2,1)S(1)}, u32[]{:S(2)}, u32[]{:S(2)}) %all-to-all-start.4) | async-done | bytes 2162720 | tf_op jit(solution)/shard_map/all_to_all | solution.py:353
  202.9 0.3 convert_reduce_fusion
  203.2 0.0 copy-start
  203.2 0.2 copy.25
  203.5 2.1 %fusion.5 = f32[1024,128]{1,0:T(8,128)} fusion(f32[4,2,128,128]{3,2,1,0:T(8,128)S(1)} %copy.25, f32[1024]{0:T(1024)S(1)} %broadcast_add_fusion, f32[1024]{0:T(1024)S(1)} %add_rsqrt_fusion.1, bf16[8192,128]{1,0:T(8,128)(2,1)} %param.6, s32[]{:T(128)S(6)} %select_n.33), kind=kLoop, calls=%fused_computation.10 | loop fusion | flops 655360 | bytes 1318916 | tf_op jit(solution)/shard_map/div | solution.py:362
  205.6 0.0 copy-done
  (6 shorter events, 0.1 us)
Async XLA Ops:
  3.0 12.5 %collective-permute-start = (bf16[32,32,128]{2,1,0:T(8,128)(2,1)S(1)}, bf16[32,32,128]{2,1,0:T(8,128)(2,1)S(1)}, u32[]{:S(2)}, u32[]{:S(2)}) collective-permute-start(bf16[32,32,128]{2,1,0:T(8,128)(2,1)S(1)} %fusion.1.refs_0_), channel_id=1, source_target_pairs={{0,16},{16,32},{32,48},{48,64},{64,80},{80,96},{96,112},{112,0},{1... | collective-permute-start | bytes 786440 | tf_op jit(solution)/shard_map/ppermute | solution.py:260
  5.5 10.0 %collective-permute-start.1 = (bf16[32,32,128]{2,1,0:T(8,128)(2,1)S(1)}, bf16[32,32,128]{2,1,0:T(8,128)(2,1)S(1)}, u32[]{:S(2)}, u32[]{:S(2)}) collective-permute-start(bf16[32,32,128]{2,1,0:T(8,128)(2,1)S(1)} %fusion.1.refs_0_), channel_id=1, source_target_pairs={{0,112},{16,0},{32,16},{48,32},{64,48},{80,64},{96,80},{112,96},{1... | collective-permute-start | bytes 786440 | tf_op jit(solution)/shard_map/ppermute | solution.py:262
  15.5 20.5 %collective-permute-start.2 = (bf16[32,32,128]{2,1,0:T(8,128)(2,1)S(1)}, bf16[32,32,128]{2,1,0:T(8,128)(2,1)S(1)}, u32[]{:S(2)}, u32[]{:S(2)}) collective-permute-start(bf16[32,32,128]{2,1,0:T(8,128)(2,1)S(1)} %collective-permute-done.refs_1_), channel_id=1, source_target_pairs={{0,16},{16,32},{32,48},{48,64},{64,80},{80,96},{96,112},{112,0},{1... | collective-permute-start | bytes 786440 | tf_op jit(solution)/shard_map/ppermute | solution.py:260
  15.5 20.5 %collective-permute-start.3 = (bf16[32,32,128]{2,1,0:T(8,128)(2,1)S(1)}, bf16[32,32,128]{2,1,0:T(8,128)(2,1)S(1)}, u32[]{:S(2)}, u32[]{:S(2)}) collective-permute-start(bf16[32,32,128]{2,1,0:T(8,128)(2,1)S(1)} %collective-permute-done.1.refs_2_), channel_id=1, source_target_pairs={{0,112},{16,0},{32,16},{48,32},{64,48},{80,64},{96,80},{112,96},{1... | collective-permute-start | bytes 786440 | tf_op jit(solution)/shard_map/ppermute | solution.py:262
  19.0 15.8 %all-to-all-start = ((s32[32,1,8]{2,1,0:T(1,128)}), s32[32,1,8]{2,1,0:T(1,128)S(1)}, u32[]{:S(2)}, u32[]{:S(2)}) async-start(s32[32,1,8]{2,1,0:T(1,128)} %bitcast.2), calls=%async_computation | async-start | bytes 32768 | tf_op jit(solution)/shard_map/all_to_all | solution.py:335
  38.0 23.2 %all-to-all-start.1 = ((bf16[32,5,32,128]{3,2,1,0:T(8,128)(2,1)}), bf16[32,5,32,128]{3,2,1,0:T(8,128)(2,1)S(1)}, u32[]{:S(2)}, u32[]{:S(2)}) async-start(bf16[32,5,32,128]{3,2,1,0:T(8,128)(2,1)} %pick.2), calls=%async_computation.1 | async-start | bytes 2621440 | tf_op jit(solution)/shard_map/all_to_all | solution.py:347
  42.4 8.9 %collective-permute-start.4 = (bf16[32,32,128]{2,1,0:T(8,128)(2,1)S(1)}, bf16[32,32,128]{2,1,0:T(8,128)(2,1)S(1)}, u32[]{:S(2)}, u32[]{:S(2)}) collective-permute-start(bf16[32,32,128]{2,1,0:T(8,128)(2,1)S(1)} %collective-permute-done.2.refs_3_), channel_id=1, source_target_pairs={{0,16},{16,32},{32,48},{48,64},{64,80},{80,96},{96,112},{112,0},{1... | collective-permute-start | bytes 786440 | tf_op jit(solution)/shard_map/ppermute | solution.py:260
  42.5 8.8 %collective-permute-start.5 = (bf16[32,32,128]{2,1,0:T(8,128)(2,1)S(1)}, bf16[32,32,128]{2,1,0:T(8,128)(2,1)S(1)}, u32[]{:S(2)}, u32[]{:S(2)}) collective-permute-start(bf16[32,32,128]{2,1,0:T(8,128)(2,1)S(1)} %collective-permute-done.3.refs_4_), channel_id=1, source_target_pairs={{0,112},{16,0},{32,16},{48,32},{64,48},{80,64},{96,80},{112,96},{1... | collective-permute-start | bytes 786440 | tf_op jit(solution)/shard_map/ppermute | solution.py:262
  51.2 7.9 %collective-permute-start.6 = (bf16[32,32,128]{2,1,0:T(8,128)(2,1)S(1)}, bf16[32,32,128]{2,1,0:T(8,128)(2,1)S(1)}, u32[]{:S(2)}, u32[]{:S(2)}) collective-permute-start(bf16[32,32,128]{2,1,0:T(8,128)(2,1)S(1)} %collective-permute-done.4.refs_0_), channel_id=1, source_target_pairs={{0,16},{16,32},{32,48},{48,64},{64,80},{80,96},{96,112},{112,0},{1... | collective-permute-start | bytes 786440 | tf_op jit(solution)/shard_map/ppermute | solution.py:260
  61.2 21.7 %all-to-all-start.2 = ((bf16[32,3,32,128]{3,2,1,0:T(8,128)(2,1)}), bf16[32,3,32,128]{3,2,1,0:T(8,128)(2,1)S(1)}, u32[]{:S(2)}, u32[]{:S(2)}) async-start(bf16[32,3,32,128]{3,2,1,0:T(8,128)(2,1)} %pick.3), calls=%async_computation.2 | async-start | bytes 1572864 | tf_op jit(solution)/shard_map/all_to_all | solution.py:347
  172.0 30.8 %all-to-all-start.4 = ((bf16[32,264,128]{2,1,0:T(8,128)(2,1)}), bf16[32,264,128]{2,1,0:T(8,128)(2,1)S(1)}, u32[]{:S(2)}, u32[]{:S(2)}) async-start(bf16[32,264,128]{2,1,0:T(8,128)(2,1)} %collect.1), calls=%async_computation.4 | async-start | bytes 4325376 | tf_op jit(solution)/shard_map/all_to_all | solution.py:353
  203.2 2.4 %copy-start = (f32[4,2,128]{2,1,0:T(2,128)}, f32[4,2,128]{2,1,0:T(2,128)S(1)}, u32[]{:S(2)}) copy-start(f32[4,2,128]{2,1,0:T(2,128)S(1)} %slice_add_fusion) | copy-start | bytes 12292

commit v3 on v2

--- a/solution.py
+++ b/solution.py
@@ -88,17 +88,21 @@
     cnt_ref[...] = jnp.zeros_like(cnt_ref)
     exp_ref[1] = jnp.zeros(exp_ref.shape[1:], exp_ref.dtype)
     inv_ref[1] = jnp.zeros(inv_ref.shape[1:], inv_ref.dtype)
-    depth = near_ref.shape[2] + far_ref.shape[2]
+    reach = near_ref.shape[1]
+    depth = reach + far_ref.shape[2]
     cores = 2
-    for first, recv_ref in ((0, near_ref), (near_ref.shape[2], far_ref)):
-        def turn(quad, carry):
-            for at in range(recv_ref.shape[2]):
-                rows = recv_ref[quad, :, at].reshape(CENT_BLK, EMBED_WIDTH)
-                slot = ((quad // cores) * depth + zpos[first + at]) * cores + quad % cores
-                cent_ref[slot] = rows.T
-            return carry
-
-        lax.fori_loop(0, near_ref.shape[0], turn, 0)
+
+    def place(quad, carry):
+        first = (quad // cores) * depth
+        for at in range(depth):
+            slot = (first + zpos[at]) * cores + quad % cores
+            if at < reach:
+                cent_ref[slot] = near_ref[quad, at]
+            else:
+                cent_ref[slot] = far_ref[quad, :, at - reach].reshape(CENT_BLK, EMBED_WIDTH).T
+        return carry
+
+    lax.fori_loop(0, near_ref.shape[0], place, 0)
 
     def spread(block, side):
         inverse = inv_ref[side]
@@ -214,6 +218,28 @@
     )(slots, ids, zpos, unit, turned, near, far)
 
 
+def turn_kernel(recv_ref, out_ref):
+    def turn(quad, carry):
+        for at in range(out_ref.shape[1]):
+            out_ref[quad, at] = recv_ref[quad, :, at].reshape(CENT_BLK, EMBED_WIDTH).T
+        return carry
+
+    lax.fori_loop(0, out_ref.shape[0], turn, 0)
+
+
+def turn_blocks(recv):
+    shape = (recv.shape[0], recv.shape[2], EMBED_WIDTH, CENT_BLK)
+    return pl.pallas_call(
+        turn_kernel,
+        out_shape=jax.ShapeDtypeStruct(shape, jnp.bfloat16),
+        in_specs=[pl.BlockSpec(memory_space=pltpu.VMEM)],
+        out_specs=pl.BlockSpec(memory_space=pltpu.VMEM),
+        compiler_params=pltpu.CompilerParams(vmem_limit_bytes=8 << 20),
+        cost_estimate=pl.CostEstimate(flops=0, transcendentals=0, bytes_accessed=recv.size * 4),
+        name="turn",
+    )(recv)
+
+
 def pick_kernel(asked, zpos, depth, *refs):
     pieces, out_ref = refs[:-1], refs[-1]
 
@@ -347,7 +373,8 @@
         recv = lax.all_to_all(picked, PLANE, split_axis=0, concat_axis=0, tiled=True)
         received.append(recv.reshape(quads, slab_count, -1, share_rows, EMBED_WIDTH))
 
-    partial = attend(group_of.reshape(-1), wanted, zpos, unit, turned, *received)
+    near, far = received
+    partial = attend(group_of.reshape(-1), wanted, zpos, unit, turned, turn_blocks(near), far)
     back = lax.all_to_all(partial, OWNER, split_axis=0, concat_axis=0, tiled=True)
     own = collect(back[:, CENT_BLK + 4, 0].astype(jnp.int32), back)
     slabs = lax.all_to_all(own, "slab", split_axis=0, concat_axis=0, tiled=True)

time: 206 us -> 206 us (level)
  no operation moved by 1% of the time
where the time goes in v3:
time: 206 us
  blocking collectives  60.4 us (29%)
  waiting for transfers between devices  56.5 us (27%)
  Pallas kernels  39.3 us (19%)
  starting transfers between devices  37.9 us (18%)
  other arithmetic  8.77 us (4%)
    all_to_all x1, blocking collectives, shards(): lax.all_to_all(partial, OWNER, split_axis=0, concat_axis=0, tiled=True)  60.4 us
    all_to_all x1, waiting for transfers between devices, shards(): slabs = lax.all_to_all(own, 'slab', split_axis=0, concat_axis=0, tiled=True)  25.7 us
    pallas_call x1, Pallas kernels, attend(): pl.pallas_call(functools.partial(attend_kernel, unroll, parts), grid_spec...  25 us
    ppermute x4, waiting for transfers between devices, gather_ring(): pieces[step] = lax.ppermute(pieces[step - 1], axis, up)  19 us
    all_to_all x2, starting transfers between devices, shards(): lax.all_to_all(picked, PLANE, split_axis=0, concat_axis=0, tiled=True)  13.1 us
    ppermute x3, starting transfers between devices, gather_ring(): pieces[-step] = lax.ppermute(pieces[1 - step], axis, down)  9.37 us
    all_to_all x1, starting transfers between devices, shards(): lax.all_to_all(requests, PLANE, split_axis=0, concat_axis=0, tiled=True)  8.9 us
    pallas_call x1, Pallas kernels, prepare(): pl.pallas_call(prepare_kernel, grid=(blocks // per_step,), in_specs=[pl.B...  6.99 us
  transfers between devices with their start and end apart: 11, of which 7 were waited for; matrix products, arithmetic and copies ran while one was open for 2% of the time, Pallas kernels for 4%

profile of v3, /device:TPU:1, one launch (start us, length us, event | category | flops | bytes accessed | tf_op | source)
XLA Modules:
  0.0 205.6 jit_solution(11446472027983799784)
XLA Ops:
  0.6 1.2 fusion
  1.8 1.2 fusion.1.refs_0_
  3.0 2.5 %collective-permute-start = (bf16[32,32,128]{2,1,0:T(8,128)(2,1)S(1)}, bf16[32,32,128]{2,1,0:T(8,128)(2,1)S(1)}, u32[]{:S(2)}, u32[]{:S(2)}) collective-permute-start(bf16[32,32,128]{2,1,0:T(8,128)(2,1)S(1)} %fusion.1.refs_0_), channel_id=1, source_target_pairs={{0,16},{16,32},{32,48},{48,64},{64,80},{80,96},{96,112},{112,0},{1... | collective-permute-start | bytes 786440 | tf_op jit(solution)/shard_map/ppermute | solution.py:286
  5.5 4.0 %collective-permute-start.1 = (bf16[32,32,128]{2,1,0:T(8,128)(2,1)S(1)}, bf16[32,32,128]{2,1,0:T(8,128)(2,1)S(1)}, u32[]{:S(2)}, u32[]{:S(2)}) collective-permute-start(bf16[32,32,128]{2,1,0:T(8,128)(2,1)S(1)} %fusion.1.refs_0_), channel_id=1, source_target_pairs={{0,112},{16,0},{32,16},{48,32},{64,48},{80,64},{96,80},{112,96},{1... | collective-permute-start | bytes 786440 | tf_op jit(solution)/shard_map/ppermute | solution.py:288
  9.6 0.7 fusion.7
  10.2 0.1 select_reduce_fusion
  10.4 5.1 %collective-permute-done.refs_1_ = bf16[32,32,128]{2,1,0:T(8,128)(2,1)S(1)} collective-permute-done((bf16[32,32,128]{2,1,0:T(8,128)(2,1)S(1)}, bf16[32,32,128]{2,1,0:T(8,128)(2,1)S(1)}, u32[]{:S(2)}, u32[]{:S(2)}) %collective-permute-start) | collective-permute-done | bytes 262176 | tf_op jit(solution)/shard_map/ppermute | solution.py:286
  15.5 0.0 collective-permute-start.2
  15.5 0.0 collective-permute-done.1.refs_2_
  15.5 2.7 %collective-permute-start.3 = (bf16[32,32,128]{2,1,0:T(8,128)(2,1)S(1)}, bf16[32,32,128]{2,1,0:T(8,128)(2,1)S(1)}, u32[]{:S(2)}, u32[]{:S(2)}) collective-permute-start(bf16[32,32,128]{2,1,0:T(8,128)(2,1)S(1)} %collective-permute-done.1.refs_2_), channel_id=1, source_target_pairs={{0,112},{16,0},{32,16},{48,32},{64,48},{80,64},{96,80},{112,96},{1... | collective-permute-start | bytes 786440 | tf_op jit(solution)/shard_map/ppermute | solution.py:288
  18.2 0.1 sub.22
  18.2 0.1 copy.24
  18.3 0.6 broadcast_in_dim.27
  19.0 8.9 %all-to-all-start = ((s32[32,1,8]{2,1,0:T(1,128)}), s32[32,1,8]{2,1,0:T(1,128)S(1)}, u32[]{:S(2)}, u32[]{:S(2)}) async-start(s32[32,1,8]{2,1,0:T(1,128)} %bitcast.2), calls=%async_computation | async-start | bytes 32768 | tf_op jit(solution)/shard_map/all_to_all | solution.py:361
  27.9 0.7 and_select_fusion.zpos
  28.5 6.2 %all-to-all-done = s32[32,1,8]{2,1,0:T(1,128)S(1)} async-done(((s32[32,1,8]{2,1,0:T(1,128)}), s32[32,1,8]{2,1,0:T(1,128)S(1)}, u32[]{:S(2)}, u32[]{:S(2)}) %all-to-all-start) | async-done | bytes 1056 | tf_op jit(solution)/shard_map/all_to_all | solution.py:361
  34.7 0.5 broadcast.78
  35.2 0.7 reduce.5
  35.9 0.1 reshape.68.asked
  36.0 0.0 collective-permute-done.2.refs_3_
  36.0 0.0 collective-permute-done.3.refs_4_
  36.0 2.0 pick.2
  38.0 4.4 %all-to-all-start.1 = ((bf16[32,5,32,128]{3,2,1,0:T(8,128)(2,1)}), bf16[32,5,32,128]{3,2,1,0:T(8,128)(2,1)S(1)}, u32[]{:S(2)}, u32[]{:S(2)}) async-start(bf16[32,5,32,128]{3,2,1,0:T(8,128)(2,1)} %pick.2), calls=%async_computation.1 | async-start | bytes 2621440 | tf_op jit(solution)/shard_map/all_to_all | solution.py:373
  42.4 0.1 collective-permute-start.4
  42.5 2.7 %collective-permute-start.5 = (bf16[32,32,128]{2,1,0:T(8,128)(2,1)S(1)}, bf16[32,32,128]{2,1,0:T(8,128)(2,1)S(1)}, u32[]{:S(2)}, u32[]{:S(2)}) collective-permute-start(bf16[32,32,128]{2,1,0:T(8,128)(2,1)S(1)} %collective-permute-done.3.refs_4_), channel_id=1, source_target_pairs={{0,112},{16,0},{32,16},{48,32},{64,48},{80,64},{96,80},{112,96},{1... | collective-permute-start | bytes 786440 | tf_op jit(solution)/shard_map/ppermute | solution.py:288
  45.1 6.1 %collective-permute-done.4.refs_0_ = bf16[32,32,128]{2,1,0:T(8,128)(2,1)S(1)} collective-permute-done((bf16[32,32,128]{2,1,0:T(8,128)(2,1)S(1)}, bf16[32,32,128]{2,1,0:T(8,128)(2,1)S(1)}, u32[]{:S(2)}, u32[]{:S(2)}) %collective-permute-start.4) | collective-permute-done | bytes 262176 | tf_op jit(solution)/shard_map/ppermute | solution.py:286
  51.2 0.0 collective-permute-start.6
  51.2 0.1 slice.19.zpos
  51.3 0.0 collective-permute-done.5.refs_1_
  51.3 7.8 %collective-permute-done.6.refs_2_ = bf16[32,32,128]{2,1,0:T(8,128)(2,1)S(1)} collective-permute-done((bf16[32,32,128]{2,1,0:T(8,128)(2,1)S(1)}, bf16[32,32,128]{2,1,0:T(8,128)(2,1)S(1)}, u32[]{:S(2)}, u32[]{:S(2)}) %collective-permute-start.6) | collective-permute-done | bytes 262176 | tf_op jit(solution)/shard_map/ppermute | solution.py:286
  59.2 1.7 pick.3
  60.9 0.3 all-to-all-done.1
  61.2 8.7 %all-to-all-start.2 = ((bf16[32,3,32,128]{3,2,1,0:T(8,128)(2,1)}), bf16[32,3,32,128]{3,2,1,0:T(8,128)(2,1)S(1)}, u32[]{:S(2)}, u32[]{:S(2)}) async-start(bf16[32,3,32,128]{3,2,1,0:T(8,128)(2,1)} %pick.3), calls=%async_computation.2 | async-start | bytes 1572864 | tf_op jit(solution)/shard_map/all_to_all | solution.py:373
  69.9 0.1 copy.23
  70.0 0.1 reshape.66.slots
  70.1 7.0 %prepare.1 = (bf16[16384,128]{1,0:T(8,128)(2,1)}, bf16[64,128,256]{2,1,0:T(8,128)(2,1)}) custom-call(bf16[16384,128]{1,0:T(8,128)(2,1)} %tok_ref), custom_call_target="tpu_custom_call" | custom-call | flops 8388608 | bytes 12582912 | tf_op jit(solution)/shard_map/prepare/pallas_call | solution.py:49
  77.1 0.6 turn.1.near_ref
  77.6 5.2 %all-to-all-done.2 = bf16[32,3,32,128]{3,2,1,0:T(8,128)(2,1)S(1)} async-done(((bf16[32,3,32,128]{3,2,1,0:T(8,128)(2,1)}), bf16[32,3,32,128]{3,2,1,0:T(8,128)(2,1)S(1)}, u32[]{:S(2)}, u32[]{:S(2)}) %all-to-all-start.2) | async-done | bytes 786464 | tf_op jit(solution)/shard_map/all_to_all | solution.py:373
  82.9 25.0 %attend.1 = bf16[32,264,128]{2,1,0:T(8,128)(2,1)S(1)} custom-call(s32[192]{0:T(256)S(1)} %reshape.66.slots, s32[32]{0:T(128)S(1)} %broadcast_add_fusion.1.ids, s32[8]{0:T(128)S(1)} %and_select_fusion.zpos, bf16[16384,128]{1,0:T(8,128)(2,1)} %get-tuple-element.6.unit_hbm, bf16[64,128,256]{2,1,0:T(8,128)(2,1)} %get-tuple-element.7.turned_hbm, ...), custom_call_target="tpu_custom_call" | custom-call | flops 6442450944 | bytes 12582912 | tf_op jit(solution)/shard_map/attend/pallas_call | solution.py:188
  107.9 60.4 %all_to_all.25.back_ref = bf16[32,264,128]{2,1,0:T(8,128)(2,1)S(1)} all-to-all(bf16[32,264,128]{2,1,0:T(8,128)(2,1)S(1)} %attend.1), channel_id=1, replica_groups=mesh['xlo'=2,'z'=8,'core'=2,'slab'=8] {'xlo','z','core'}, dimensions={0} | all-to-all | bytes 4325376 | tf_op jit(solution)/shard_map/all_to_all | solution.py:378
  168.4 0.7 fusion.6.asked
  169.0 3.0 %collect.1 = bf16[32,264,128]{2,1,0:T(8,128)(2,1)} custom-call(s32[32]{0:T(128)S(1)} %fusion.6.asked, bf16[32,264,128]{2,1,0:T(8,128)(2,1)S(1)} %all_to_all.25.back_ref), custom_call_target="tpu_custom_call" | custom-call | flops 1081344 | bytes 4325376 | tf_op jit(solution)/shard_map/collect/pallas_call | solution.py:316
  172.0 3.9 %all-to-all-start.4 = ((bf16[32,264,128]{2,1,0:T(8,128)(2,1)}), bf16[32,264,128]{2,1,0:T(8,128)(2,1)S(1)}, u32[]{:S(2)}, u32[]{:S(2)}) async-start(bf16[32,264,128]{2,1,0:T(8,128)(2,1)} %collect.1), calls=%async_computation.4 | async-start | bytes 4325376 | tf_op jit(solution)/shard_map/all_to_all | solution.py:380
  176.0 1.2 fusion.2
  177.1 25.7 %all-to-all-done.4 = bf16[32,264,128]{2,1,0:T(8,128)(2,1)S(1)} async-done(((bf16[32,264,128]{2,1,0:T(8,128)(2,1)}), bf16[32,264,128]{2,1,0:T(8,128)(2,1)S(1)}, u32[]{:S(2)}, u32[]{:S(2)}) %all-to-all-start.4) | async-done | bytes 2162720 | tf_op jit(solution)/shard_map/all_to_all | solution.py:380
  202.9 0.3 convert_reduce_fusion
  203.2 0.0 copy-start
  203.2 0.2 copy.25
  203.5 2.1 %fusion.5 = f32[1024,128]{1,0:T(8,128)} fusion(f32[4,2,128,128]{3,2,1,0:T(8,128)S(1)} %copy.25, f32[1024]{0:T(1024)S(1)} %broadcast_add_fusion, f32[1024]{0:T(1024)S(1)} %add_rsqrt_fusion.1, bf16[8192,128]{1,0:T(8,128)(2,1)} %param.6, s32[]{:T(128)S(6)} %select_n.33), kind=kLoop, calls=%fused_computation.10 | loop fusion | flops 655360 | bytes 1318916 | tf_op jit(solution)/shard_map/div | solution.py:389
  205.6 0.0 copy-done
  (6 shorter events, 0.1 us)
Async XLA Ops:
  3.0 12.5 %collective-permute-start = (bf16[32,32,128]{2,1,0:T(8,128)(2,1)S(1)}, bf16[32,32,128]{2,1,0:T(8,128)(2,1)S(1)}, u32[]{:S(2)}, u32[]{:S(2)}) collective-permute-start(bf16[32,32,128]{2,1,0:T(8,128)(2,1)S(1)} %fusion.1.refs_0_), channel_id=1, source_target_pairs={{0,16},{16,32},{32,48},{48,64},{64,80},{80,96},{96,112},{112,0},{1... | collective-permute-start | bytes 786440 | tf_op jit(solution)/shard_map/ppermute | solution.py:286
  5.5 10.0 %collective-permute-start.1 = (bf16[32,32,128]{2,1,0:T(8,128)(2,1)S(1)}, bf16[32,32,128]{2,1,0:T(8,128)(2,1)S(1)}, u32[]{:S(2)}, u32[]{:S(2)}) collective-permute-start(bf16[32,32,128]{2,1,0:T(8,128)(2,1)S(1)} %fusion.1.refs_0_), channel_id=1, source_target_pairs={{0,112},{16,0},{32,16},{48,32},{64,48},{80,64},{96,80},{112,96},{1... | collective-permute-start | bytes 786440 | tf_op jit(solution)/shard_map/ppermute | solution.py:288
  15.5 20.5 %collective-permute-start.2 = (bf16[32,32,128]{2,1,0:T(8,128)(2,1)S(1)}, bf16[32,32,128]{2,1,0:T(8,128)(2,1)S(1)}, u32[]{:S(2)}, u32[]{:S(2)}) collective-permute-start(bf16[32,32,128]{2,1,0:T(8,128)(2,1)S(1)} %collective-permute-done.refs_1_), channel_id=1, source_target_pairs={{0,16},{16,32},{32,48},{48,64},{64,80},{80,96},{96,112},{112,0},{1... | collective-permute-start | bytes 786440 | tf_op jit(solution)/shard_map/ppermute | solution.py:286
  15.5 20.5 %collective-permute-start.3 = (bf16[32,32,128]{2,1,0:T(8,128)(2,1)S(1)}, bf16[32,32,128]{2,1,0:T(8,128)(2,1)S(1)}, u32[]{:S(2)}, u32[]{:S(2)}) collective-permute-start(bf16[32,32,128]{2,1,0:T(8,128)(2,1)S(1)} %collective-permute-done.1.refs_2_), channel_id=1, source_target_pairs={{0,112},{16,0},{32,16},{48,32},{64,48},{80,64},{96,80},{112,96},{1... | collective-permute-start | bytes 786440 | tf_op jit(solution)/shard_map/ppermute | solution.py:288
  19.0 15.8 %all-to-all-start = ((s32[32,1,8]{2,1,0:T(1,128)}), s32[32,1,8]{2,1,0:T(1,128)S(1)}, u32[]{:S(2)}, u32[]{:S(2)}) async-start(s32[32,1,8]{2,1,0:T(1,128)} %bitcast.2), calls=%async_computation | async-start | bytes 32768 | tf_op jit(solution)/shard_map/all_to_all | solution.py:361
  38.0 23.2 %all-to-all-start.1 = ((bf16[32,5,32,128]{3,2,1,0:T(8,128)(2,1)}), bf16[32,5,32,128]{3,2,1,0:T(8,128)(2,1)S(1)}, u32[]{:S(2)}, u32[]{:S(2)}) async-start(bf16[32,5,32,128]{3,2,1,0:T(8,128)(2,1)} %pick.2), calls=%async_computation.1 | async-start | bytes 2621440 | tf_op jit(solution)/shard_map/all_to_all | solution.py:373
  42.4 8.9 %collective-permute-start.4 = (bf16[32,32,128]{2,1,0:T(8,128)(2,1)S(1)}, bf16[32,32,128]{2,1,0:T(8,128)(2,1)S(1)}, u32[]{:S(2)}, u32[]{:S(2)}) collective-permute-start(bf16[32,32,128]{2,1,0:T(8,128)(2,1)S(1)} %collective-permute-done.2.refs_3_), channel_id=1, source_target_pairs={{0,16},{16,32},{32,48},{48,64},{64,80},{80,96},{96,112},{112,0},{1... | collective-permute-start | bytes 786440 | tf_op jit(solution)/shard_map/ppermute | solution.py:286
  42.5 8.8 %collective-permute-start.5 = (bf16[32,32,128]{2,1,0:T(8,128)(2,1)S(1)}, bf16[32,32,128]{2,1,0:T(8,128)(2,1)S(1)}, u32[]{:S(2)}, u32[]{:S(2)}) collective-permute-start(bf16[32,32,128]{2,1,0:T(8,128)(2,1)S(1)} %collective-permute-done.3.refs_4_), channel_id=1, source_target_pairs={{0,112},{16,0},{32,16},{48,32},{64,48},{80,64},{96,80},{112,96},{1... | collective-permute-start | bytes 786440 | tf_op jit(solution)/shard_map/ppermute | solution.py:288
  51.2 7.9 %collective-permute-start.6 = (bf16[32,32,128]{2,1,0:T(8,128)(2,1)S(1)}, bf16[32,32,128]{2,1,0:T(8,128)(2,1)S(1)}, u32[]{:S(2)}, u32[]{:S(2)}) collective-permute-start(bf16[32,32,128]{2,1,0:T(8,128)(2,1)S(1)} %collective-permute-done.4.refs_0_), channel_id=1, source_target_pairs={{0,16},{16,32},{32,48},{48,64},{64,80},{80,96},{96,112},{112,0},{1... | collective-permute-start | bytes 786440 | tf_op jit(solution)/shard_map/ppermute | solution.py:286
  61.2 21.7 %all-to-all-start.2 = ((bf16[32,3,32,128]{3,2,1,0:T(8,128)(2,1)}), bf16[32,3,32,128]{3,2,1,0:T(8,128)(2,1)S(1)}, u32[]{:S(2)}, u32[]{:S(2)}) async-start(bf16[32,3,32,128]{3,2,1,0:T(8,128)(2,1)} %pick.3), calls=%async_computation.2 | async-start | bytes 1572864 | tf_op jit(solution)/shard_map/all_to_all | solution.py:373
  172.0 30.8 %all-to-all-start.4 = ((bf16[32,264,128]{2,1,0:T(8,128)(2,1)}), bf16[32,264,128]{2,1,0:T(8,128)(2,1)S(1)}, u32[]{:S(2)}, u32[]{:S(2)}) async-start(bf16[32,264,128]{2,1,0:T(8,128)(2,1)} %collect.1), calls=%async_computation.4 | async-start | bytes 4325376 | tf_op jit(solution)/shard_map/all_to_all | solution.py:380
  203.2 2.4 %copy-start = (f32[4,2,128]{2,1,0:T(2,128)}, f32[4,2,128]{2,1,0:T(2,128)S(1)}, u32[]{:S(2)}) copy-start(f32[4,2,128]{2,1,0:T(2,128)S(1)} %slice_add_fusion) | copy-start | bytes 12292
